TPU v7x, 128 devices: a whole 4x4x4 slice. The times are simulated.
128 devices in a mesh: dp: 4 (over y_lo, core), tp: 32 (over y_hi, z, x).
Axes of the slice: x: 4, y: 4 (y_hi: 2, y_lo: 2; y = y_hi * 2 + y_lo), z: 4, core: 2. Of those that a mesh axis runs over, the one named last changes fastest.
Arguments:
- teacher_partial: bfloat16 [32, 512, 4608], P('tp', 'dp'), may hold values from -6 to 6
- teacher_residual: bfloat16 [512, 4608], P(('dp', 'tp')), may hold values from -120 to 120
- post_gain: float32 [4608], replicated, may hold values from 0.5 to 1.5
- final_gain: float32 [4608], replicated, may hold values from 0.5 to 1.5
- teacher_head: bfloat16 [4608, 131072], P(None, ('dp', 'tp')), may hold values from -40 to 40
- student_hidden: bfloat16 [512, 3584], P(('dp', 'tp')), may hold values from -120 to 120
- student_gain: float32 [3584], replicated, may hold values from 0.5 to 1.5
- student_head: bfloat16 [3584, 131072], P(None, ('dp', 'tp')), may hold values from -40 to 40
- labels: int32 [512], P('dp'), may hold values from 0 to 131071
- lengths: int32 [4, 8], P('dp'), may hold values from 1 to 48, 96 in all within a row
Outputs:
- grad_hidden: float32 [512, 3584], P(('dp', 'tp'))
- token_loss: float32 [512], P(('dp', 'tp'))
Inputs may be any that keep to these rules, and one draw needn't show every extreme that they name: `lengths`: group g's 8 sequences fill, in order, its first 96 rows; its remaining 128 - 96 rows are padding.
All inputs are finite; a program needn't handle non-finite values.
Results may differ from a plain program's by a relative error of at most 0.03.
Values may be sent and summed in bfloat16 or wider, within the bound.
A program may use at most 128 MiB of HBM per device.

v0:
```python
import jax
import jax.numpy as jnp
from jax import lax
from jax.sharding import Mesh
from jax.sharding import PartitionSpec as P

TP = ("tp_0", "tp_1", "tp_2")
DP = ("dp_0", "dp_1")
DP_TP = ("dp_0", "dp_1", "tp_0", "tp_1", "tp_2")


EPS = 1e-06
BETA = 0.5
LOSS_SCALE = 1024.0


def cut_along(value, dim, peers):
    before, after = (value.shape[:dim], value.shape[dim + 1 :])
    return jnp.moveaxis(value.reshape(*before, peers, -1, *after), dim, 0)


def sent_and_summed(value, axis, dim):
    peers = lax.axis_size(axis)
    parts = lax.all_to_all(cut_along(value, dim, peers), axis, 0, 0, tiled=True)
    return jnp.sum(parts.astype(jnp.float32), axis=0)


def side_by_side(arrays, axis, dim, along):
    widths = [a.shape[along] for a in arrays]
    both = jnp.concatenate(arrays, axis=along)
    out = lax.all_gather(both, axis, axis=dim, tiled=True)
    return tuple(jnp.split(out, [sum(widths[:k]) for k in range(1, len(widths))], axis=along))


def all_in_one(value, axis):
    leaves = jax.tree.leaves(value)
    turns = sorted(range(len(leaves)), key=lambda k: -leaves[k].size)
    width = (1, *leaves[turns[0]].shape)[-1]
    lines = [
        jnp.pad(leaves[k].reshape(-1), (0, -leaves[k].size % width)).reshape(-1, width)
        for k in turns
    ]
    both, at, found = (lax.all_gather(jnp.concatenate(lines), axis), 0, {})
    for k, line in zip(turns, lines):
        slab = both[:, at : at + len(line)].reshape(len(both), -1)
        found[k] = slab[:, : leaves[k].size].reshape(-1, *leaves[k].shape)
        at += len(line)
    numbers = iter(range(len(leaves)))
    return jax.tree.map(lambda _: found[next(numbers)], value)


def combined_by_axis(value, axes, combine):
    for axis in axes:
        pieces = all_in_one(value, axis)
        value = jax.tree.map(lambda part: part[0], pieces)
        for k in range(1, lax.axis_size(axis)):
            value = combine(value, jax.tree.map(lambda part: part[k], pieces))
    return value


def norm_rows(values, gain):
    inverse = lax.rsqrt(jnp.mean(values * values, axis=-1, keepdims=True) + EPS)
    return (values * inverse * gain, inverse)


def token_weights(lengths, tok_rows):
    ends = jnp.cumsum(lengths, axis=1)
    starts = ends - lengths
    places = jnp.arange(tok_rows, dtype=jnp.int32)
    inside = (places[None, :, None] >= starts[:, None, :]) & (
        places[None, :, None] < ends[:, None, :]
    )
    spans = jnp.sum(jnp.where(inside, lengths[:, None, :], 0), axis=2)
    covered = jnp.sum(inside.astype(jnp.int32), axis=2)
    return covered.astype(jnp.float32) / jnp.maximum(spans, 1).astype(jnp.float32)


def merge_stats(first, second):
    t_max = jnp.maximum(first[0], second[0])
    t_one = jnp.exp(first[0] - t_max)
    t_two = jnp.exp(second[0] - t_max)
    s_max = jnp.maximum(first[3], second[3])
    s_one = jnp.exp(first[3] - s_max)
    s_two = jnp.exp(second[3] - s_max)
    return (
        t_max,
        first[1] * t_one + second[1] * t_two,
        first[2] * t_one + second[2] * t_two,
        s_max,
        first[4] * s_one + second[4] * s_two,
        first[5] + second[5],
    )


def shards(
    teacher_partial,
    teacher_residual,
    post_gain,
    final_gain,
    teacher_head,
    student_hidden,
    student_gain,
    student_head,
    labels,
    lengths,
):
    share = teacher_residual.shape[0]
    tok_rows = labels.shape[0]
    mlp_sum = sent_and_summed(teacher_partial[0].astype(jnp.float32).astype(jnp.bfloat16), TP, 0)
    post, unused = norm_rows(mlp_sum, post_gain)
    final = teacher_residual.astype(jnp.float32) + post
    teacher_norm = norm_rows(final, final_gain)[0].astype(jnp.bfloat16)
    student_f = student_hidden.astype(jnp.float32)
    student_scaled, inverse = norm_rows(student_f, student_gain)
    student_norm = student_scaled.astype(jnp.bfloat16)
    label_all, length_all = (
        lax.all_gather(labels, DP, axis=0, tiled=True),
        lax.all_gather(lengths, DP, axis=0, tiled=True),
    )
    groups = length_all.shape[0]
    weight_all = token_weights(length_all, tok_rows)
    whole_t, whole_s = side_by_side((teacher_norm, student_norm), DP_TP, 0, 1)
    label_rows = label_all.reshape(groups, tok_rows).reshape(-1)
    weight_rows = weight_all.reshape(-1)
    vocab_dev = teacher_head.shape[1]
    position = lax.axis_index(DP) * lax.axis_size(TP) + lax.axis_index(TP)
    columns = position * vocab_dev + jnp.arange(vocab_dev, dtype=jnp.int32)
    t_logits = jnp.dot(whole_t, teacher_head, preferred_element_type=jnp.float32)
    s_logits = jnp.dot(whole_s, student_head, preferred_element_type=jnp.float32)
    hit = label_rows[:, None] == columns[None, :]
    label_logit = jnp.sum(jnp.where(hit, s_logits, 0.0), axis=1)
    t_local = jnp.max(t_logits, axis=1)
    s_local = jnp.max(s_logits, axis=1)
    t_exp = jnp.exp(t_logits - t_local[:, None])
    s_exp = jnp.exp(s_logits - s_local[:, None])
    t_max, t_total, t_cross, s_max, s_total, label_value = combined_by_axis(
        (
            t_local,
            jnp.sum(t_exp, axis=1),
            jnp.sum(t_exp * (t_logits - s_logits), axis=1),
            s_local,
            jnp.sum(s_exp, axis=1),
            label_logit,
        ),
        DP_TP,
        merge_stats,
    )
    t_exp = t_exp * jnp.exp(t_local - t_max)[:, None]
    s_exp = s_exp * jnp.exp(s_local - s_max)[:, None]
    t_log = t_max + jnp.log(t_total)
    s_log = s_max + jnp.log(s_total)
    divergence = t_cross / t_total - t_log + s_log
    label_term = s_log - label_value
    row_loss = jnp.where(weight_rows > 0, divergence + BETA * label_term, 0.0)
    t_prob = t_exp / t_total[:, None]
    s_prob = s_exp / s_total[:, None]
    scale = (LOSS_SCALE * weight_rows)[:, None]
    logit_grad = (scale * ((1.0 + BETA) * s_prob - t_prob - BETA * hit.astype(jnp.float32))).astype(
        jnp.bfloat16
    )
    summed = lax.psum_scatter(
        lax.dot_general(
            logit_grad, student_head, (((1,), (1,)), ((), ())), preferred_element_type=jnp.float32
        ),
        DP_TP,
        scatter_dimension=0,
        tiled=True,
    )
    scaled = summed * student_gain
    inner = jnp.mean(scaled * student_f, axis=1, keepdims=True)
    grad_hidden = inverse * scaled - student_f * (inverse * inverse * inverse) * inner
    token_loss = lax.dynamic_slice_in_dim(row_loss, position * share, share, 0)
    return (grad_hidden, token_loss)


def solution(mesh):
    torus = Mesh(mesh.devices.reshape(2, 2, 2, 4, 4), ("dp_0", "dp_1", "tp_0", "tp_1", "tp_2"))
    return jax.shard_map(
        shards,
        mesh=torus,
        in_specs=(
            P(TP, DP, None),
            P(DP_TP, None),
            P(),
            P(),
            P(None, DP_TP),
            P(DP_TP, None),
            P(),
            P(None, DP_TP),
            P(DP),
            P(DP, None),
        ),
        out_specs=(P(DP_TP, None), P(DP_TP)),
        check_vma=False,
    )
```

profile of v0, /device:TPU:0, one launch (start us, length us, event | category | flops | bytes accessed | tf_op | source)
XLA Modules:
  0.0 595.5 jit_solution(10907730072785063472)
XLA Ops:
  7.2 2.2 reshape.1547
  9.4 11.0 %all-to-all-start = ((bf16[32,4,4608]{2,1,0:T(4,128)(2,1)}), bf16[32,4,4608]{2,1,0:T(4,128)(2,1)S(1)}, u32[]{:S(2)}, u32[]{:S(2)}) async-start(bf16[32,4,4608]{2,1,0:T(4,128)(2,1)} %reshape.1547), calls=%async_computation | async-start | bytes 2359296 | tf_op jit(solution)/shard_map/all_to_all | solution.py:24
  20.8 19.2 %all-to-all-done = bf16[32,4,4608]{2,1,0:T(4,128)(2,1)S(1)} async-done(((bf16[32,4,4608]{2,1,0:T(4,128)(2,1)}), bf16[32,4,4608]{2,1,0:T(4,128)(2,1)S(1)}, u32[]{:S(2)}, u32[]{:S(2)}) %all-to-all-start) | async-done | bytes 1179680 | tf_op jit(solution)/shard_map/all_to_all | solution.py:24
  40.0 0.5 convert_reduce_fusion
  40.7 0.2 multiply_reduce_fusion.1
  41.0 0.7 maximum_bitcast_fusion
  41.8 5.0 all-gather.5
  46.8 0.2 reduce_window_sum.11
  47.0 5.0 all-gather.7
  52.1 295.3 %all-gather.15.cloned.1.call-done = bf16[128,4,8192]{2,1,0:T(4,128)(2,1)} async-done(((bf16[1,4,8192]{2,1,0:T(4,128)(2,1)}), bf16[128,4,8192]{2,1,0:T(4,128)(2,1)}) %all-gather.15.cloned.1.call-update) | async-done | bytes 8388624 | tf_op jit(solution)/shard_map/all_gather | solution.py:31
  347.4 12.5 %reshape.1562 = bf16[512,8192]{1,0:T(8,128)(2,1)} reshape(bf16[128,4,8192]{2,1,0:T(4,128)(2,1)} %all-gather.15.cloned.1.call-done) | data formatting | bytes 16777216
  359.9 9.3 %fusion.116 = (f32[512]{0:T(512)S(1)}, f32[512,1024]{1,0:T(8,128)S(1)}) fusion(bf16[4608,1024]{1,0:T(8,128)(2,1)} %param.14, bf16[512,8192]{1,0:T(8,128)(2,1)} %reshape.1562), kind=kOutput, calls=%fused_computation.217 | convolution fusion | flops 4832361984 | bytes 16254976 | tf_op jit(solution)/shard_map/dot_general | solution.py:128
  369.2 6.3 %fusion.117 = (f32[512]{0:T(512)S(1)}, f32[512,1024]{1,0:T(8,128)S(1)}) fusion(bf16[3584,1024]{1,0:T(8,128)(2,1)} %param.17, bf16[512,8192]{1,0:T(8,128)(2,1)S(1)} %copy-done), kind=kOutput, calls=%fused_computation.218 | convolution fusion | flops 3758620160 | bytes 13109248 | tf_op jit(solution)/shard_map/dot_general | solution.py:129
  375.6 1.6 multiply_reduce_fusion
  377.2 4.4 all-gather.8
  381.7 2.7 all-gather.9
  384.5 5.9 all-gather.10
  390.6 12.0 %all-gather.11 = f32[4,6,512]{2,1,0:T(8,128)S(1)} all-gather(f32[1,6,512]{2,1,0:T(8,128)S(1)} %bitcast.469), channel_id=5, replica_groups=mesh['dp_0'=2,'dp_1'=2,'tp_0'=2,'tp_1'=4,'tp_2'=4] {'tp_1'}, dimensions={0}, use_global_device_ids=true | all-gather | bytes 61440 | tf_op jit(solution)/shard_map/all_gather | solution.py:43
  402.7 12.1 %all-gather.12 = f32[4,6,512]{2,1,0:T(8,128)S(1)} all-gather(f32[1,6,512]{2,1,0:T(8,128)S(1)} %bitcast.470), channel_id=6, replica_groups=mesh['dp_0'=2,'dp_1'=2,'tp_0'=2,'tp_1'=4,'tp_2'=4] {'tp_2'}, dimensions={0}, use_global_device_ids=true | all-gather | bytes 61440 | tf_op jit(solution)/shard_map/all_gather | solution.py:43
  414.9 11.8 %fusion.10 = f32[512,3584]{1,0:T(8,128)} fusion(bf16[3584,1024]{1,0:T(8,128)(2,1)} %param.17, f32[512,1024]{1,0:T(8,128)S(1)} %get-tuple-element.64, f32[512,1024]{1,0:T(8,128)} %copy-done.1, f32[512]{0:T(512)S(1)} %get-tuple-element.11, f32[512]{0:T(512)S(1)} %get-tuple-element.67, f32[512]{0:T(512)S(1)} %get-tuple-element.9, ...), kind=kOutput, calls=%fused_computation.16 | convolution fusion | flops 3764912128 | bytes 18894848 | tf_op jit(solution)/shard_map/dot_general | solution.py:162
  426.8 0.6 dynamic_slice.3
  427.4 158.6 %all-reduce.3.cloned.1.call-done = f32[512,3584]{1,0:T(8,128)} async-done(((f32[512,3584]{1,0:T(8,128)}), f32[512,3584]{1,0:T(8,128)}) %all-reduce.3.cloned.1.call-update) | async-done | bytes 7340048
  586.0 1.0 fusion.29
  587.0 1.6 fusion.28
  (57 shorter events, 1.3 us)
Async XLA Ops:
  7.2 13.3 %copy-start.2 = (bf16[4,3584]{1,0:T(4,128)(2,1)S(1)}, bf16[4,3584]{1,0:T(4,128)(2,1)}, u32[]{:S(2)}) copy-start(bf16[4,3584]{1,0:T(4,128)(2,1)} %param.15) | copy-start | bytes 86020
  7.2 13.5 %copy-start.3 = (f32[3584]{0:T(1024)S(1)}, f32[3584]{0:T(1024)}, u32[]{:S(2)}) copy-start(f32[3584]{0:T(1024)} %param.16) | copy-start | bytes 43012
  9.4 31.2 %copy-start.4 = (bf16[4,4608]{1,0:T(4,128)(2,1)S(1)}, bf16[4,4608]{1,0:T(4,128)(2,1)}, u32[]{:S(2)}) copy-start(bf16[4,4608]{1,0:T(4,128)(2,1)} %param.11) | copy-start | bytes 110596
  9.4 31.2 %copy-start.5 = (f32[4608]{0:T(1024)S(1)}, f32[4608]{0:T(1024)}, u32[]{:S(2)}) copy-start(f32[4608]{0:T(1024)} %param.12) | copy-start | bytes 55300
  9.4 31.5 %copy-start.6 = (f32[4608]{0:T(1024)S(1)}, f32[4608]{0:T(1024)}, u32[]{:S(2)}) copy-start(f32[4608]{0:T(1024)} %param.13) | copy-start | bytes 55300
  9.4 32.3 %copy-start.7 = (s32[1,8]{1,0:T(1,128)S(1)}, s32[1,8]{1,0:T(1,128)}, u32[]{:S(2)}) copy-start(s32[1,8]{1,0:T(1,128)} %param.19) | copy-start | bytes 100
  9.4 37.6 %copy-start.8 = (s32[128]{0:T(128)S(1)}, s32[128]{0:T(128)}, u32[]{:S(2)}) copy-start(s32[128]{0:T(128)} %param.18) | copy-start | bytes 1540
  9.4 30.6 %all-to-all-start = ((bf16[32,4,4608]{2,1,0:T(4,128)(2,1)}), bf16[32,4,4608]{2,1,0:T(4,128)(2,1)S(1)}, u32[]{:S(2)}, u32[]{:S(2)}) async-start(bf16[32,4,4608]{2,1,0:T(4,128)(2,1)} %reshape.1547), calls=%async_computation | async-start | bytes 2359296 | tf_op jit(solution)/shard_map/all_to_all | solution.py:24
  20.5 326.9 %all-gather.15.cloned.1.call-start = ((), (), s32[]{:S(2)}) async-start(), calls=%async_computation.1 | async-start | bytes 8454144 | tf_op jit(solution)/shard_map/all_gather | solution.py:31
  41.7 544.3 %all-reduce.3.cloned.1.call-start = ((), (), s32[]{:S(2)}) async-start(), calls=%async_computation.2 | async-start | bytes 14680064
  359.9 9.3 %copy-start = (bf16[512,8192]{1,0:T(8,128)(2,1)S(1)}, bf16[512,8192]{1,0:T(8,128)(2,1)}, u32[]{:S(2)}) copy-start(bf16[512,8192]{1,0:T(8,128)(2,1)} %reshape.1562) | copy-start | bytes 25165828
  375.6 1.6 copy-start.1
Sparse Core Ops, SparseCore 0:
  41.8 305.5 all-gather.14
  426.9 159.0 all-reduce.2
where the time goes:
time: 597 us; the launch traced here: 595 us
  waiting for transfers between devices  473 us (79%)
  blocking collectives  47.2 us (8%)
  matrix products  27.4 us (5%)
  local copies, waits for them, and re-layouts  15.5 us (3%)
  between operations  14.3 us (2%)
  starting transfers between devices  11.1 us (2%)
  other arithmetic  6.73 us (1%)
    all_gather x1, waiting for transfers between devices, side_by_side(): out = lax.all_gather(both, axis, axis=dim, tiled=True)  295 us
    unnamed x3, waiting for transfers between devices  159 us
    all_gather x5, blocking collectives, all_in_one(): both, at, found = (lax.all_gather(jnp.concatenate(lines), axis), 0, {})  37.2 us
    all_to_all x1, waiting for transfers between devices, sent_and_summed(): parts = lax.all_to_all(cut_along(value, dim, peers), axis, 0, 0, tiled=True)  19.2 us
    unnamed x19, local copies, waits for them, and re-layouts  12.5 us
  transfers between devices with their start and end apart: 3, of which 3 were waited for; matrix products, arithmetic and copies ran while one was open for 0% of the time, Pallas kernels for 0%

commit v1 on v0

v1 whole, which is shorter than its diff:
```python
import functools

import jax
import jax.numpy as jnp
from jax import lax
from jax.experimental import pallas as pl
from jax.experimental.pallas import tpu as pltpu
from jax.sharding import Mesh
from jax.sharding import PartitionSpec as P

TP = ("tp_0", "tp_1", "tp_2")
DP = ("dp_0", "dp_1")
DP_TP = ("dp_0", "dp_1", "tp_0", "tp_1", "tp_2")
MESH = pl.DeviceIdType.MESH

EPS = 1e-06
BETA = 0.5
LOSS_SCALE = 1024.0

F32 = jnp.float32
BF16 = jnp.bfloat16

D_T = 4608
D_S = 3584
QT = D_T // 4
QS = D_S // 4
VOC = 1024
ROWS = 384
NSEQ = 8
LANES = 128

PARTS_T = ((0, 384, "xyz"), (384, 384, "yzx"), (768, 384, "zxy"))
PARTS_S = ((0, 256, "xyz"), (256, 384, "yzx"), (640, 256, "zxy"))
PARTS_G = ((0, 256, "zyx"), (256, 384, "xzy"), (640, 256, "yxz"))


def live_pieces():
    first = [(c, y, z) for c in range(2) for y in range(2) for z in range(4)]
    second = [(c, y, z) for c in range(2) for y in range(2, 4) for z in range(2)]
    return first + second


PIECES = live_pieces()


class Place:
    def __init__(self):
        self.c = lax.axis_index("dp_1")
        self.z = lax.axis_index("tp_1")
        self.x = lax.axis_index("tp_2")
        self.y_lo = lax.axis_index("dp_0")
        self.y_hi = lax.axis_index("tp_0")
        self.y = self.y_hi * 2 + self.y_lo

    def at(self, axis):
        return {"x": self.x, "y": self.y, "z": self.z}[axis]

    def shifted(self, axis, k):
        return lax.rem(self.at(axis) + k, 4)

    def along(self, axis, to):
        y_lo, y_hi, z, x = (self.y_lo, self.y_hi, self.z, self.x)
        if axis == "x":
            x = to
        elif axis == "z":
            z = to
        else:
            y_lo, y_hi = lax.rem(to, 2), lax.div(to, 2)
        return (y_lo, self.c, y_hi, z, x)

    def sibling(self):
        return (self.y_lo, 1 - self.c, self.y_hi, self.z, self.x)


def remote(src, dst, send, recv, to):
    return pltpu.make_async_remote_copy(
        src_ref=src, dst_ref=dst, send_sem=send, recv_sem=recv, device_id=to, device_id_type=MESH
    )


def kernel(
    partial_ref,
    residual_ref,
    post_ref,
    final_ref,
    t_head_ref,
    hidden_ref,
    s_gain_ref,
    s_head_ref,
    labels_ref,
    lengths_ref,
    grad_ref,
    loss_ref,
    w_t,
    w_s,
    rb,
    tb,
    sb,
    res_out,
    res_in,
    stu_out,
    stu_in,
    asm_t,
    asm_s,
    mean_out,
    mean_in,
    tab_own,
    tab,
    lab_col,
    wgt_col,
    t_log,
    s_log,
    lg,
    stat,
    stat_in,
    back,
    loss_blk,
    g,
    core_in,
    rr,
    ng_out,
    ng_in,
    sem_w,
    a_send,
    a_recv,
    a_own,
    x_send,
    x_recv,
    tab_send,
    tab_recv,
    ag_send,
    ag_recv,
    sib_send,
    sib_recv,
    st_send,
    st_recv,
    rs_send,
    rs_recv,
):
    me = Place()
    tp = me.y_hi * 16 + me.z * 4 + me.x
    dp = me.y_lo * 2 + me.c
    position = dp * 32 + tp

    load_s = pltpu.make_async_copy(s_head_ref, w_s, sem_w.at[0])
    load_t = pltpu.make_async_copy(t_head_ref, w_t, sem_w.at[1])
    load_s.start()
    load_t.start()

    barrier = pltpu.get_barrier_semaphore()

    def tp_device(p):
        return (me.y_lo, me.c, lax.div(p, 16), lax.rem(lax.div(p, 4), 4), lax.rem(p, 4))

    @pl.loop(1, 32)
    def _(k):
        pl.semaphore_signal(
            barrier, inc=1, device_id=tp_device(lax.rem(tp + k, 32)), device_id_type=MESH
        )

    other = (1 - me.y_lo, 1 - me.c, me.y_hi, me.z, me.x)
    for to in (
        me.along("y", me.shifted("y", 1)),
        me.along("y", me.shifted("y", 3)),
        me.sibling(),
        other,
    ):
        pl.semaphore_signal(barrier, inc=1, device_id=to, device_id_type=MESH)
    pl.semaphore_wait(barrier, 35)

    def a_copy(k, peer):
        rows = pl.ds(pl.multiple_of(lax.div(peer, 4) * 16, 16), 16)
        cols = pl.ds(pl.multiple_of(lax.rem(peer, 4) * QT, 128), QT)
        return remote(
            partial_ref.at[0, rows, cols], rb.at[k], a_send.at[k], a_recv.at[k], tp_device(peer)
        )

    own_rows = pl.ds(pl.multiple_of(lax.div(tp, 4) * 16, 16), 16)
    own_cols = pl.ds(pl.multiple_of(me.x * QT, 128), QT)
    own_copy = pltpu.make_async_copy(partial_ref.at[0, own_rows, own_cols], rb.at[0], a_own)
    own_copy.start()

    @pl.loop(1, 32)
    def _(k):
        a_copy(k, lax.rem(tp + k, 32)).start()

    hidden = hidden_ref[...].astype(F32)
    inverse = lax.rsqrt(jnp.mean(hidden * hidden, axis=-1, keepdims=True) + EPS)
    student = (hidden * inverse * s_gain_ref[...]).astype(BF16)
    residual = residual_ref[...]
    for q in range(4):
        stu_out[q] = student[:, q * QS : (q + 1) * QS]
        res_out[q] = residual[:, q * QT : (q + 1) * QT]
    stu_in[me.x] = stu_out[me.x]
    res_in[me.x] = res_out[me.x]

    def x_copy(kind, src, dst, k):
        to = me.shifted("x", k)
        return remote(
            src.at[to],
            dst.at[me.x],
            x_send.at[kind, k - 1],
            x_recv.at[kind, k - 1],
            me.along("x", to),
        )

    def x_arrival(kind, src, dst, k):
        frm = me.shifted("x", 4 - k)
        return remote(
            src.at[frm],
            dst.at[frm],
            x_send.at[kind, k - 1],
            x_recv.at[kind, k - 1],
            me.along("x", frm),
        )

    for k in (1, 2, 3):
        x_copy(0, stu_out, stu_in, k).start()
        x_copy(1, res_out, res_in, k).start()

    lane = lax.broadcasted_iota(jnp.int32, (1, LANES), 1)
    start = jnp.int32(0)
    weight = jnp.zeros((1, LANES), F32)
    for i in range(NSEQ):
        length = lengths_ref[0, i]
        end = start + length
        inside = (lane >= start) & (lane < end)
        share = 1.0 / jnp.full((1, LANES), length, jnp.int32).astype(F32)
        weight = jnp.where(inside, share, weight)
        start = end
    sub = lax.broadcasted_iota(jnp.int32, (8, LANES), 0)
    label_row = labels_ref[...].astype(F32)
    tab_own[...] = jnp.where(
        sub == 0,
        jnp.broadcast_to(label_row, (8, LANES)),
        jnp.where(sub == 1, jnp.broadcast_to(weight, (8, LANES)), 0.0),
    )
    tab[dp] = tab_own[...]
    dp_peers = ((0, 1), (1, 0), (1, 1))

    def tab_copy(n):
        dy, dc = dp_peers[n]
        y_lo = 1 - me.y_lo if dy else me.y_lo
        c = 1 - me.c if dc else me.c
        to = (y_lo, c, me.y_hi, me.z, me.x)
        return (
            remote(tab_own, tab.at[dp], tab_send.at[n], tab_recv.at[n], to),
            remote(tab_own, tab.at[y_lo * 2 + c], tab_send.at[n], tab_recv.at[n], to),
        )

    for n in range(3):
        tab_copy(n)[0].start()

    def box(buf, axis, to, done, lo, width):
        where = []
        for a in "yzx":
            if a == axis:
                where.append(pl.ds(to, 1))
            elif a in done:
                where.append(pl.ds(0, 4))
            else:
                where.append(pl.ds(me.at(a), 1))
        return buf.at[me.c, where[0], where[1], where[2], :, pl.ds(lo, width)]

    def gather(which, buf, parts, stage):
        out = []
        for p, (lo, width, order) in enumerate(parts):
            axis, done = order[stage], order[:stage]
            own = box(buf, axis, me.at(axis), done, lo, width)
            for k in (1, 2, 3):
                sems = (ag_send.at[which, stage, p, k - 1], ag_recv.at[which, stage, p, k - 1])
                frm = me.shifted(axis, 4 - k)
                theirs = box(buf, axis, frm, done, lo, width)
                out.append(
                    (
                        remote(own, own, *sems, me.along(axis, me.shifted(axis, k))),
                        remote(theirs, theirs, *sems, me.along(axis, frm)),
                    )
                )
        return out

    def start_all(copies):
        for sent, unused in copies:
            sent.start()

    def arrive_all(copies):
        for unused, arrived in copies:
            arrived.wait_recv()

    def sent_all(copies):
        for sent, unused in copies:
            sent.wait_send()

    def swap(which, buf):
        out = []
        for n, (y, z) in enumerate(((pl.ds(0, 2), pl.ds(0, 4)), (pl.ds(2, 2), pl.ds(0, 2)))):
            sems = (sib_send.at[which, n], sib_recv.at[which, n])
            own, theirs = buf.at[me.c, y, z], buf.at[1 - me.c, y, z]
            out.append(
                (remote(own, own, *sems, me.sibling()), remote(theirs, theirs, *sems, me.sibling()))
            )
        return out

    student_stages = [gather(1, sb, PARTS_S, s) for s in range(3)]
    teacher_stages = [gather(0, tb, PARTS_T, s) for s in range(3)]
    student_swap, teacher_swap = swap(1, sb), swap(0, tb)

    for k in (1, 2, 3):
        x_arrival(0, stu_out, stu_in, k).wait_recv()
    for i in range(4):
        asm_s[4 * i : 4 * i + 4, :] = stu_in[i].astype(F32)
    sb[me.c, me.y, me.z, me.x] = asm_s[...].astype(BF16)
    start_all(student_stages[0])

    own_copy.wait()
    total = rb[0].astype(F32)

    def add_one(k, acc):
        frm = lax.rem(tp + 32 - k, 32)
        a_copy(k, frm).wait_recv()
        return acc + rb[k].astype(F32)

    total = lax.fori_loop(1, 32, add_one, total)

    def row_total(n, part):
        mean_out[n] = jnp.broadcast_to(part, (16, LANES))
        mean_in[n, me.x] = mean_out[n]
        copies = []
        for k in (1, 2, 3):
            to, frm = me.shifted("x", k), me.shifted("x", 4 - k)
            sems = (x_send.at[2 + n, k - 1], x_recv.at[2 + n, k - 1])
            copies.append(
                (
                    remote(mean_out.at[n], mean_in.at[n, me.x], *sems, me.along("x", to)),
                    remote(mean_out.at[n], mean_in.at[n, frm], *sems, me.along("x", frm)),
                )
            )
        start_all(copies)
        return copies

    def row_mean(n, copies):
        arrive_all(copies)
        whole = mean_in[n, 0] + mean_in[n, 1] + mean_in[n, 2] + mean_in[n, 3]
        return whole[:, 0:1] / D_T

    first_mean = row_total(0, jnp.sum(total * total, axis=1, keepdims=True))
    arrive_all(student_stages[0])
    start_all(student_stages[1])
    for k in (1, 2, 3):
        x_arrival(1, res_out, res_in, k).wait_recv()
    for i in range(4):
        asm_t[4 * i : 4 * i + 4, :] = res_in[i].astype(F32)
    post = total * lax.rsqrt(row_mean(0, first_mean) + EPS) * post_ref[:, own_cols]
    final = asm_t[...] + post
    second_mean = row_total(1, jnp.sum(final * final, axis=1, keepdims=True))
    arrive_all(student_stages[1])
    start_all(student_stages[2])
    normed = final * lax.rsqrt(row_mean(1, second_mean) + EPS) * final_ref[:, own_cols]
    tb[me.c, me.y, me.z, me.x] = normed.astype(BF16)
    start_all(teacher_stages[0])

    for n in range(3):
        tab_copy(n)[1].wait_recv()
    for group in range(4):
        table = tab[group]
        for row, col in ((0, lab_col), (1, wgt_col)):
            turned = jnp.broadcast_to(table[row : row + 1, :], (LANES, LANES)).T
            for m, (c, y, z) in enumerate(PIECES):
                if (y % 2) * 2 + c == group:
                    j = (y // 2) * 4 + z
                    col[m * 16 : (m + 1) * 16, :] = turned[j * 16 : (j + 1) * 16, :]
    g[:, 2:4, 2:4] = jnp.zeros((2, 2, 2, 4, 16, QS), BF16)
    loss_blk[:, 2:4, 2:4] = jnp.zeros((2, 2, 2, 16, LANES), F32)

    arrive_all(teacher_stages[0])
    start_all(teacher_stages[1])
    arrive_all(student_stages[2])
    start_all(student_swap)
    arrive_all(teacher_stages[1])
    start_all(teacher_stages[2])

    def live_rows(buf, q, width):
        return jnp.concatenate(
            [
                buf[:, 0:2, :, q].reshape(256, width),
                buf[:, 2:4, 0:2, q].reshape(128, width),
            ],
            axis=0,
        )

    def logits(buf, head, out, width):
        @pl.loop(0, VOC // 256)
        def _(n):
            cols = pl.ds(pl.multiple_of(n * 256, 256), 256)
            acc = None
            for q in range(4):
                term = jnp.dot(
                    live_rows(buf, q, width),
                    head[q * width : (q + 1) * width, cols],
                    preferred_element_type=F32,
                )
                acc = term if acc is None else acc + term
            out[:, cols] = acc

    arrive_all(student_swap)
    load_s.wait()
    logits(sb, w_s, s_log, QS)
    arrive_all(teacher_stages[2])
    start_all(teacher_swap)
    load_t.wait()
    arrive_all(teacher_swap)
    logits(tb, w_t, t_log, QT)

    first_col = (position * VOC).astype(F32)

    def columns():
        return lax.broadcasted_iota(jnp.int32, (32, VOC), 1).astype(F32) + first_col

    lanes = lax.broadcasted_iota(jnp.int32, (32, LANES), 1)

    @pl.loop(0, ROWS // 32)
    def _(r):
        rows = pl.ds(pl.multiple_of(r * 32, 32), 32)
        t, s = t_log[rows, :], s_log[rows, :]
        t_max = jnp.max(t, axis=1, keepdims=True)
        s_max = jnp.max(s, axis=1, keepdims=True)
        t_exp = jnp.exp(t - t_max)
        t_sum = jnp.sum(t_exp, axis=1, keepdims=True)
        cross = jnp.sum(t_exp * (t - s), axis=1, keepdims=True)
        s_sum = jnp.sum(jnp.exp(s - s_max), axis=1, keepdims=True)
        hit = columns() == lab_col[rows, 0:1]
        value = jnp.sum(jnp.where(hit, s, 0.0), axis=1, keepdims=True)
        held = wgt_col[rows, :]
        for n, one in enumerate((t_max, t_sum, cross, s_max, s_sum, value)):
            held = jnp.where(lanes == n, one, held)
        back[rows, :] = held

    for i in range(3):
        turned = back[i * 128 : (i + 1) * 128, :].T
        stat[0, :, i * 128 : (i + 1) * 128] = turned[0:8, :]

    def merged(values):
        t_max = functools.reduce(jnp.maximum, [v[0:1] for v in values])
        s_max = functools.reduce(jnp.maximum, [v[3:4] for v in values])
        t_sum = cross = s_sum = label = 0.0
        for v in values:
            t_one = jnp.exp(v[0:1] - t_max)
            s_one = jnp.exp(v[3:4] - s_max)
            t_sum += v[1:2] * t_one
            cross += v[2:3] * t_one
            s_sum += v[4:5] * s_one
            label += v[5:6]
        return [t_max, t_sum, cross, s_max, s_sum, label, values[0][6:7]]

    stat_copies = []
    for n, axis in enumerate("cxyz"):
        copies = []
        for k in (1,) if axis == "c" else (1, 2, 3):
            sems = (st_send.at[n, k - 1], st_recv.at[n, k - 1])
            dst = stat_in.at[n, k - 1]
            to = me.sibling() if axis == "c" else me.along(axis, me.shifted(axis, k))
            copy = remote(stat.at[n], dst, *sems, to)
            copies.append((copy, copy))
        start_all(copies)
        stat_copies += copies
        arrive_all(copies)
        values = [stat[n]] + [stat_in[n, k] for k in range(len(copies))]
        for i, line in enumerate(merged(values)):
            stat[n + 1, i : i + 1, :] = line

    end = stat[4]
    t_whole = end[0:1] + jnp.log(end[1:2])
    s_whole = end[3:4] + jnp.log(end[4:5])
    divergence = end[2:3] / end[1:2] - t_whole + s_whole
    row_loss = jnp.where(end[6:7] > 0, divergence + BETA * (s_whole - end[5:6]), 0.0)
    sub = lax.broadcasted_iota(jnp.int32, (8, ROWS), 0)
    lines = jnp.zeros((8, ROWS), F32)
    for n, one in enumerate((t_whole, s_whole, row_loss)):
        lines = jnp.where(sub == n, jnp.broadcast_to(one, (8, ROWS)), lines)
    for i in range(3):
        tall = jnp.concatenate(
            [lines[:, i * 128 : (i + 1) * 128], jnp.zeros((120, LANES), F32)], axis=0
        )
        back[i * 128 : (i + 1) * 128, :] = tall.T
    for m, (c, y, z) in enumerate(PIECES):
        loss_blk[c, y, z] = jnp.broadcast_to(back[m * 16 : (m + 1) * 16, 2:3], (16, LANES))

    @pl.loop(0, ROWS // 32)
    def _(r):
        rows = pl.ds(pl.multiple_of(r * 32, 32), 32)
        t_prob = jnp.exp(t_log[rows, :] - back[rows, 0:1])
        s_prob = jnp.exp(s_log[rows, :] - back[rows, 1:2])
        hit = (columns() == lab_col[rows, 0:1]).astype(F32)
        scale = LOSS_SCALE * wgt_col[rows, 0:1]
        lg[rows, :] = (scale * ((1.0 + BETA) * s_prob - t_prob - BETA * hit)).astype(BF16)

    for q in range(4):
        for lo in range(0, QS, 128 * 7):
            width = min(128 * 7, QS - lo)
            share = lax.dot_general(
                lg[...],
                w_s[q * QS + lo : q * QS + lo + width, :],
                (((1,), (1,)), ((), ())),
                preferred_element_type=F32,
            ).astype(BF16)
            g[:, 0:2, :, q, :, lo : lo + width] = share[0:256].reshape(2, 2, 4, 16, width)
            g[:, 2:4, 0:2, q, :, lo : lo + width] = share[256:384].reshape(2, 2, 2, 16, width)

    core_copies = []
    for n, (y, z) in enumerate(((pl.ds(0, 2), pl.ds(0, 4)), (pl.ds(2, 2), pl.ds(0, 2)))):
        copy = remote(
            g.at[1 - me.c, y, z],
            core_in.at[y, z],
            sib_send.at[2, n],
            sib_recv.at[2, n],
            me.sibling(),
        )
        core_copies.append((copy, copy))
    start_all(core_copies)
    arrive_all(core_copies)
    for ys, zs in (((0, 1), 4), ((2, 3), 2)):
        for y in ys:

            @pl.loop(0, zs * 4)
            def _(i, y=y):
                z, x = lax.div(i, 4), lax.rem(i, 4)
                both = g[me.c, y, z, x].astype(F32) + core_in[y, z, x].astype(F32)
                g[me.c, y, z, x] = both.astype(BF16)

    totals = []
    for stage in range(3):
        made = []
        for p, (lo, width, order) in enumerate(PARTS_G):
            axis, left = order[stage], order[stage + 1 :]
            for k in (1, 2, 3):
                to = me.shifted(axis, k)
                copy = remote(
                    box(g, axis, to, left, lo, width),
                    rr[stage][p].at[k - 1],
                    rs_send.at[stage, p, k - 1],
                    rs_recv.at[stage, p, k - 1],
                    me.along(axis, to),
                )
                made.append((copy, copy))
        start_all(made)
        arrive_all(made)
        core_copies += made
        for p, (lo, width, order) in enumerate(PARTS_G):
            left = order[stage + 1 :]
            came = rr[stage][p]

            def summed(y, z, x, i, j, k):
                whole = g[me.c, y, z, x, :, lo : lo + width].astype(F32)
                for n in range(3):
                    whole = whole + came[n, i, j, k].astype(F32)
                return whole

            if stage == 2:
                whole = summed(me.y, me.z, me.x, 0, 0, 0)
                for i in range(4):
                    ng_out[i, :, lo : lo + width] = whole[4 * i : 4 * i + 4]
            else:

                @pl.loop(0, 4 ** len(left))
                def _(n, left=left, lo=lo, width=width, summed=summed):
                    at = {a: me.at(a) for a in "yzx"}
                    slot = {a: 0 for a in "yzx"}
                    for a in left:
                        at[a] = slot[a] = lax.rem(n, 4)
                        n = lax.div(n, 4)
                    whole = summed(at["y"], at["z"], at["x"], slot["y"], slot["z"], slot["x"])
                    g[me.c, at["y"], at["z"], at["x"], :, lo : lo + width] = whole.astype(BF16)

    ng_in[me.x] = ng_out[me.x]
    for k in (1, 2, 3):
        x_copy(4, ng_out, ng_in, k).start()

    losses = loss_blk[me.c, me.y, me.z]
    mine = jnp.zeros((4, LANES), F32)
    for i in range(4):
        mine = jnp.where(me.x == i, losses[4 * i : 4 * i + 4], mine)
    diagonal = lax.broadcasted_iota(jnp.int32, (4, LANES), 0) == lax.broadcasted_iota(
        jnp.int32, (4, LANES), 1
    )
    loss_ref[...] = jnp.sum(jnp.where(diagonal, mine, 0.0), axis=0, keepdims=True)

    for k in (1, 2, 3):
        x_arrival(4, ng_out, ng_in, k).wait_recv()
    norm_grad = jnp.concatenate([ng_in[q] for q in range(4)], axis=1)
    live = me.y_hi * 4 + me.z < 6
    scaled = norm_grad * s_gain_ref[...]
    inner = jnp.mean(scaled * hidden, axis=1, keepdims=True)
    grad = inverse * scaled - hidden * (inverse * inverse * inverse) * inner
    grad_ref[...] = jnp.where(live, grad, 0.0)

    @pl.loop(1, 32)
    def _(k):
        a_copy(k, lax.rem(tp + k, 32)).wait_send()

    for k in (1, 2, 3):
        x_copy(0, stu_out, stu_in, k).wait_send()
        x_copy(1, res_out, res_in, k).wait_send()
        x_copy(4, ng_out, ng_in, k).wait_send()
    for n in range(3):
        tab_copy(n)[0].wait_send()
    sent_all(first_mean + second_mean)
    for copies in student_stages + teacher_stages + [student_swap, teacher_swap]:
        sent_all(copies)
    sent_all(stat_copies + core_copies)


def scratch():
    dma = pltpu.SemaphoreType.DMA
    vm = pltpu.VMEM
    rr = []
    for stage in range(3):
        row = []
        for lo, width, order in PARTS_G:
            spots = [4 if a in order[stage + 1 :] else 1 for a in "yzx"]
            row.append(vm((3, *spots, 16, width), BF16))
        rr.append(tuple(row))
    return {
        "w_t": vm((D_T, VOC), BF16),
        "w_s": vm((D_S, VOC), BF16),
        "rb": vm((32, 16, QT), BF16),
        "tb": vm((2, 4, 4, 4, 16, QT), BF16),
        "sb": vm((2, 4, 4, 4, 16, QS), BF16),
        "res_out": vm((4, 4, QT), BF16),
        "res_in": vm((4, 4, QT), BF16),
        "stu_out": vm((4, 4, QS), BF16),
        "stu_in": vm((4, 4, QS), BF16),
        "asm_t": vm((16, QT), F32),
        "asm_s": vm((16, QS), F32),
        "mean_out": vm((2, 16, LANES), F32),
        "mean_in": vm((2, 4, 16, LANES), F32),
        "tab_own": vm((8, LANES), F32),
        "tab": vm((4, 8, LANES), F32),
        "lab_col": vm((ROWS, LANES), F32),
        "wgt_col": vm((ROWS, LANES), F32),
        "t_log": vm((ROWS, VOC), F32),
        "s_log": vm((ROWS, VOC), F32),
        "lg": vm((ROWS, VOC), BF16),
        "stat": vm((5, 8, ROWS), F32),
        "stat_in": vm((4, 3, 8, ROWS), F32),
        "back": vm((ROWS, LANES), F32),
        "loss_blk": vm((2, 4, 4, 16, LANES), F32),
        "g": vm((2, 4, 4, 4, 16, QS), BF16),
        "core_in": vm((4, 4, 4, 16, QS), BF16),
        "rr": tuple(rr),
        "ng_out": vm((4, 4, QS), F32),
        "ng_in": vm((4, 4, QS), F32),
        "sem_w": dma((2,)),
        "a_send": dma((32,)),
        "a_recv": dma((32,)),
        "a_own": dma(()),
        "x_send": dma((5, 3)),
        "x_recv": dma((5, 3)),
        "tab_send": dma((3,)),
        "tab_recv": dma((3,)),
        "ag_send": dma((2, 3, 3, 3)),
        "ag_recv": dma((2, 3, 3, 3)),
        "sib_send": dma((3, 2)),
        "sib_recv": dma((3, 2)),
        "st_send": dma((4, 3)),
        "st_recv": dma((4, 3)),
        "rs_send": dma((3, 3, 3)),
        "rs_recv": dma((3, 3, 3)),
    }


def shards(
    teacher_partial,
    teacher_residual,
    post_gain,
    final_gain,
    teacher_head,
    student_hidden,
    student_gain,
    student_head,
    labels,
    lengths,
):
    whole = pl.BlockSpec(memory_space=pltpu.VMEM)
    place = pl.BlockSpec(memory_space=pl.ANY)
    spaces = scratch()
    names = list(spaces)
    leaves, tree = jax.tree.flatten([spaces[n] for n in names])

    def body(*refs):
        held = jax.tree.unflatten(tree, refs[12:])
        kernel(*refs[:12], **dict(zip(names, held)))

    grad, loss = pl.pallas_call(
        body,
        out_shape=(
            jax.ShapeDtypeStruct((4, D_S), F32),
            jax.ShapeDtypeStruct((1, LANES), F32),
        ),
        in_specs=[
            place,
            whole,
            whole,
            whole,
            place,
            whole,
            whole,
            place,
            whole,
            pl.BlockSpec(memory_space=pltpu.SMEM),
        ],
        out_specs=(whole, whole),
        scratch_shapes=leaves,
        compiler_params=pltpu.CompilerParams(
            collective_id=0, has_side_effects=True, vmem_limit_bytes=60 * 2**20
        ),
        name="distill",
    )(
        teacher_partial,
        teacher_residual,
        post_gain.reshape(1, -1),
        final_gain.reshape(1, -1),
        teacher_head,
        student_hidden,
        student_gain.reshape(1, -1),
        student_head,
        labels.reshape(1, -1),
        lengths,
    )
    return grad, loss[0, :4]


def solution(mesh):
    torus = Mesh(mesh.devices.reshape(2, 2, 2, 4, 4), ("dp_0", "dp_1", "tp_0", "tp_1", "tp_2"))
    return jax.shard_map(
        shards,
        mesh=torus,
        in_specs=(
            P(TP, DP, None),
            P(DP_TP, None),
            P(),
            P(),
            P(None, DP_TP),
            P(DP_TP, None),
            P(),
            P(None, DP_TP),
            P(DP),
            P(DP, None),
        ),
        out_specs=(P(DP_TP, None), P(DP_TP)),
        check_vma=False,
    )
```

time: 597 us -> 123 us (0.21)
  waiting for transfers between devices: 473 us -> 0 us
  Pallas kernels: 0 us -> 115 us
  blocking collectives: 47.2 us -> 0 us
  matrix products: 27.4 us -> 0 us
  between operations: 14.3 us -> 0.64 us
  starting transfers between devices: 11.1 us -> 0 us
  local copies, waits for them, and re-layouts: 15.5 us -> 6.57 us
  other arithmetic: 6.73 us -> 0 us
    all_gather x1 -> x0, waiting for transfers between devices: 295 us -> none  [side_by_side(): out = lax.all_gather(both, axis, axis=dim, tiled=True)]
    unnamed x3 -> x0, waiting for transfers between devices: 159 us -> none
    pallas_call x0 -> x1, Pallas kernels: none -> 115 us  [shards(): pl.pallas_call(body, out_shape=(jax.ShapeDtypeStruct((4, D_S), F32), jax....]
    all_gather x7 -> x0, blocking collectives: 47.2 us -> none  [the longest x5 37.2 us: all_in_one(): both, at, found = (lax.all_gather(jnp.concatenate(lines), axis), 0, {})]
    dot_general x3 -> x0, matrix products: 27.4 us -> none  [the longest x1 11.8 us: shards(): lax.dot_general(logit_grad, student_head, (((1,), (1,)), ((), ())), prefe...]
    all_to_all x1 -> x0, waiting for transfers between devices: 19.2 us -> none  [sent_and_summed(): parts = lax.all_to_all(cut_along(value, dim, peers), axis, 0, 0, tiled=True)]
    unnamed x19 -> x1, local copies, waits for them, and re-layouts: 12.5 us -> 1.44 us
    all_to_all x1 -> x0, starting transfers between devices: 11 us -> none  [sent_and_summed(): parts = lax.all_to_all(cut_along(value, dim, peers), axis, 0, 0, tiled=True)]
  transfers between devices with their start and end apart: 3 -> 0, of which waited for: 3 -> 0; matrix products, arithmetic and copies ran while one was open for 0% -> 0% of each run, Pallas kernels for 0% -> 0%
where the time goes in v1:
time: 123 us
  Pallas kernels  115 us (93%)
  local copies, waits for them, and re-layouts  6.57 us (5%)
    pallas_call x1, Pallas kernels, shards(): pl.pallas_call(body, out_shape=(jax.ShapeDtypeStruct((4, D_S), F32), jax....  115 us

profile of v1, /device:TPU:0, one launch (start us, length us, event | category | flops | bytes accessed | tf_op | source)
XLA Modules:
  0.0 122.6 jit_solution(14220234726662824807)
XLA Ops:
  0.6 1.3 %reshape.18.refs_6_ = f32[1,3584]{1,0:T(1,128)} reshape(f32[3584]{0:T(1024)} %param.16) | data formatting | bytes 28672 | tf_op jit(solution)/shard_map/reshape | solution.py:724
  2.0 1.3 %reshape.16.refs_2_ = f32[1,4608]{1,0:T(1,128)} reshape(f32[4608]{0:T(1024)} %param.12) | data formatting | bytes 36864 | tf_op jit(solution)/shard_map/reshape | solution.py:720
  3.3 1.3 %reshape.17.refs_3_ = f32[1,4608]{1,0:T(1,128)} reshape(f32[4608]{0:T(1024)} %param.13) | data formatting | bytes 36864 | tf_op jit(solution)/shard_map/reshape | solution.py:721
  4.7 115.4 %distill.1 = (f32[4,3584]{1,0:T(4,128)}, f32[1,128]{1,0:T(1,128)}) custom-call(bf16[1,128,4608]{2,1,0:T(8,128)(2,1)} %refs_0_.1, bf16[4,4608]{1,0:T(4,128)(2,1)} %refs_1_.1, f32[1,4608]{1,0:T(1,128)} %reshape.16.refs_2_, f32[1,4608]{1,0:T(1,128)} %reshape.17.refs_3_, bf16[4608,1024]{1,0:T(8,128)(2,1)} %refs_4_.1, bf16[4,3584]{1,0:T(4,128)(2,1)} %refs_5_.1, ...), custom_call_target="tpu_custom_call" | custom-call | tf_op jit(solution)/shard_map/distill/pallas_call | solution.py:693
  120.0 1.1 slice_bitcast_fusion
  121.1 1.4 %copy.13 = f32[4,3584]{1,0:T(4,128)} copy(f32[4,3584]{1,0:T(4,128)} %get-tuple-element.8) | data formatting | bytes 114688

commit v2 on v1

--- a/solution.py
+++ b/solution.py
@@ -1,4 +1,5 @@
 import functools
+import itertools
 
 import jax
 import jax.numpy as jnp
@@ -26,18 +27,22 @@
 QS = D_S // 4
 VOC = 1024
 ROWS = 384
+HALF = 192
 NSEQ = 8
 LANES = 128
 
-PARTS_T = ((0, 384, "xyz"), (384, 384, "yzx"), (768, 384, "zxy"))
+PARTS_A = ((0, 384, "x", "hz"), (384, 384, "z", "hx"), (768, 384, "h", "zx"))
+PARTS_T = ((0, 384, "x", "y", "z"), (384, 384, "x", "z", "y"), (768, 384, "", "yz", "x"))
 PARTS_S = ((0, 256, "xyz"), (256, 384, "yzx"), (640, 256, "zxy"))
 PARTS_G = ((0, 256, "zyx"), (256, 384, "xzy"), (640, 256, "yxz"))
 
 
 def live_pieces():
-    first = [(c, y, z) for c in range(2) for y in range(2) for z in range(4)]
-    second = [(c, y, z) for c in range(2) for y in range(2, 4) for z in range(2)]
-    return first + second
+    held = []
+    for c in range(2):
+        held += [(c, y, z) for y in range(2) for z in range(4)]
+        held += [(c, y, z) for y in range(2, 4) for z in range(2)]
+    return held
 
 
 PIECES = live_pieces()
@@ -53,20 +58,28 @@
         self.y = self.y_hi * 2 + self.y_lo
 
     def at(self, axis):
-        return {"x": self.x, "y": self.y, "z": self.z}[axis]
+        return {"x": self.x, "y": self.y, "z": self.z, "h": self.y_hi}[axis]
 
     def shifted(self, axis, k):
-        return lax.rem(self.at(axis) + k, 4)
+        return lax.rem(self.at(axis) + k, 2 if axis == "h" else 4)
+
+    def to(self, **spots):
+        y_lo, y_hi = self.y_lo, self.y_hi
+        if "y" in spots:
+            y_lo, y_hi = lax.rem(spots["y"], 2), lax.div(spots["y"], 2)
+        y_hi = spots.get("h", y_hi)
+        return (y_lo, self.c, y_hi, spots.get("z", self.z), spots.get("x", self.x))
 
     def along(self, axis, to):
-        y_lo, y_hi, z, x = (self.y_lo, self.y_hi, self.z, self.x)
-        if axis == "x":
-            x = to
-        elif axis == "z":
-            z = to
-        else:
-            y_lo, y_hi = lax.rem(to, 2), lax.div(to, 2)
-        return (y_lo, self.c, y_hi, z, x)
+        return self.to(**{axis: to})
+
+    def offsets(self, axes):
+        sizes = [2 if a == "h" else 4 for a in axes]
+        for ks in itertools.product(*[range(n) for n in sizes]):
+            if any(ks):
+                sent = {a: self.shifted(a, k) for a, k in zip(axes, ks)}
+                heard = {a: self.shifted(a, n - k) for a, k, n in zip(axes, ks, sizes)}
+                yield (sent, heard)
 
     def sibling(self):
         return (self.y_lo, 1 - self.c, self.y_hi, self.z, self.x)
@@ -93,17 +106,18 @@
     loss_ref,
     w_t,
     w_s,
-    rb,
+    pb,
+    first_in,
+    second_in,
+    rows_in,
     tb,
     sb,
-    res_out,
     res_in,
     stu_out,
     stu_in,
     asm_t,
     asm_s,
-    mean_out,
-    mean_in,
+    normed,
     tab_own,
     tab,
     lab_col,
@@ -121,9 +135,11 @@
     ng_out,
     ng_in,
     sem_w,
-    a_send,
-    a_recv,
     a_own,
+    f_send,
+    f_recv,
+    h_send,
+    h_recv,
     x_send,
     x_recv,
     tab_send,
@@ -147,52 +163,70 @@
     load_s.start()
     load_t.start()
 
+    own_copies = []
+    for q in range(4):
+        copy = pltpu.make_async_copy(
+            partial_ref.at[:, :, :, pl.ds(q * QT, QT)], pb.at[:, :, q], a_own.at[q]
+        )
+        copy.start()
+        own_copies.append(copy)
+
     barrier = pltpu.get_barrier_semaphore()
-
-    def tp_device(p):
-        return (me.y_lo, me.c, lax.div(p, 16), lax.rem(lax.div(p, 4), 4), lax.rem(p, 4))
-
-    @pl.loop(1, 32)
-    def _(k):
-        pl.semaphore_signal(
-            barrier, inc=1, device_id=tp_device(lax.rem(tp + k, 32)), device_id_type=MESH
-        )
-
-    other = (1 - me.y_lo, 1 - me.c, me.y_hi, me.z, me.x)
-    for to in (
-        me.along("y", me.shifted("y", 1)),
-        me.along("y", me.shifted("y", 3)),
-        me.sibling(),
-        other,
-    ):
+    near = [me.to(**sent) for sent, heard in me.offsets("yz")]
+    near += [me.along("x", me.shifted("x", k)) for k in (1, 2, 3)]
+    for k in (1, 2, 3):
+        near += [me.to(x=me.shifted("x", k), z=me.shifted("z", n)) for n in (1, 2, 3)]
+        near += [me.to(x=me.shifted("x", k), h=1 - me.y_hi)]
+    near += [me.sibling(), (1 - me.y_lo, 1 - me.c, me.y_hi, me.z, me.x)]
+    for to in near:
         pl.semaphore_signal(barrier, inc=1, device_id=to, device_id_type=MESH)
-    pl.semaphore_wait(barrier, 35)
-
-    def a_copy(k, peer):
-        rows = pl.ds(pl.multiple_of(lax.div(peer, 4) * 16, 16), 16)
-        cols = pl.ds(pl.multiple_of(lax.rem(peer, 4) * QT, 128), QT)
-        return remote(
-            partial_ref.at[0, rows, cols], rb.at[k], a_send.at[k], a_recv.at[k], tp_device(peer)
-        )
-
-    own_rows = pl.ds(pl.multiple_of(lax.div(tp, 4) * 16, 16), 16)
-    own_cols = pl.ds(pl.multiple_of(me.x * QT, 128), QT)
-    own_copy = pltpu.make_async_copy(partial_ref.at[0, own_rows, own_cols], rb.at[0], a_own)
-    own_copy.start()
-
-    @pl.loop(1, 32)
-    def _(k):
-        a_copy(k, lax.rem(tp + k, 32)).start()
+    pl.semaphore_wait(barrier, len(near))
+
+    opened = []
+
+    def start_all(copies):
+        for sent, unused in copies:
+            sent.start()
+        opened.extend(copies)
+
+    def arrive_all(copies):
+        for unused, arrived in copies:
+            arrived.wait_recv()
+
+    for copy in own_copies:
+        copy.wait()
+
+    def pb_box(spots, lo, width):
+        where = [pl.ds(spots[a], 1) if a in spots else slice(None) for a in "hzx"]
+        return pb.at[where[0], where[1], where[2], :, pl.ds(lo, width)]
+
+    first_stage, second_stage = [], []
+    for p, (lo, width, axis, plane) in enumerate(PARTS_A):
+        for n, (sent, heard) in enumerate(me.offsets(axis)):
+            copy = remote(
+                pb_box(sent, lo, width),
+                first_in[p].at[n],
+                f_send.at[p, n],
+                f_recv.at[p, n],
+                me.to(**sent),
+            )
+            first_stage.append((copy, copy))
+        for n, (sent, heard) in enumerate(me.offsets(plane)):
+            spots = {axis: me.at(axis), **sent}
+            src = pb.at[spots["h"], spots["z"], spots["x"], :, pl.ds(lo, width)]
+            copy = remote(
+                src, second_in[p].at[n], h_send.at[p, n], h_recv.at[p, n], me.to(**sent)
+            )
+            second_stage.append((copy, copy))
 
     hidden = hidden_ref[...].astype(F32)
+    s_gain = s_gain_ref[...].reshape(1, D_S)
     inverse = lax.rsqrt(jnp.mean(hidden * hidden, axis=-1, keepdims=True) + EPS)
-    student = (hidden * inverse * s_gain_ref[...]).astype(BF16)
-    residual = residual_ref[...]
+    student = (hidden * inverse * s_gain).astype(BF16)
     for q in range(4):
         stu_out[q] = student[:, q * QS : (q + 1) * QS]
-        res_out[q] = residual[:, q * QT : (q + 1) * QT]
     stu_in[me.x] = stu_out[me.x]
-    res_in[me.x] = res_out[me.x]
+    res_in[me.x] = residual_ref[...]
 
     def x_copy(kind, src, dst, k):
         to = me.shifted("x", k)
@@ -216,7 +250,23 @@
 
     for k in (1, 2, 3):
         x_copy(0, stu_out, stu_in, k).start()
-        x_copy(1, res_out, res_in, k).start()
+    start_all(first_stage)
+
+    def spread(kind, own, where):
+        copies = []
+        for k in (1, 2, 3):
+            frm = me.shifted("x", 4 - k)
+            sems = (x_send.at[kind, k - 1], x_recv.at[kind, k - 1])
+            copies.append(
+                (
+                    remote(own, where(me.x), *sems, me.along("x", me.shifted("x", k))),
+                    remote(own, where(frm), *sems, me.along("x", frm)),
+                )
+            )
+        return copies
+
+    residual_copies = spread(1, residual_ref, lambda i: res_in.at[i])
+    start_all(residual_copies)
 
     lane = lax.broadcasted_iota(jnp.int32, (1, LANES), 1)
     start = jnp.int32(0)
@@ -251,45 +301,29 @@
     for n in range(3):
         tab_copy(n)[0].start()
 
-    def box(buf, axis, to, done, lo, width):
+    def box(buf, spots, done, lo, width):
         where = []
         for a in "yzx":
-            if a == axis:
-                where.append(pl.ds(to, 1))
-            elif a in done:
-                where.append(pl.ds(0, 4))
-            else:
-                where.append(pl.ds(me.at(a), 1))
+            where.append(pl.ds(0, 4) if a in done else pl.ds(spots.get(a, me.at(a)), 1))
         return buf.at[me.c, where[0], where[1], where[2], :, pl.ds(lo, width)]
 
     def gather(which, buf, parts, stage):
         out = []
         for p, (lo, width, order) in enumerate(parts):
             axis, done = order[stage], order[:stage]
-            own = box(buf, axis, me.at(axis), done, lo, width)
-            for k in (1, 2, 3):
-                sems = (ag_send.at[which, stage, p, k - 1], ag_recv.at[which, stage, p, k - 1])
-                frm = me.shifted(axis, 4 - k)
-                theirs = box(buf, axis, frm, done, lo, width)
-                out.append(
-                    (
-                        remote(own, own, *sems, me.along(axis, me.shifted(axis, k))),
-                        remote(theirs, theirs, *sems, me.along(axis, frm)),
-                    )
-                )
+            out += one_part(which, buf, stage, p, lo, width, axis, done)
         return out
 
-    def start_all(copies):
-        for sent, unused in copies:
-            sent.start()
-
-    def arrive_all(copies):
-        for unused, arrived in copies:
-            arrived.wait_recv()
-
-    def sent_all(copies):
-        for sent, unused in copies:
-            sent.wait_send()
+    def one_part(which, buf, stage, p, lo, width, axes, done):
+        out = []
+        own = box(buf, {}, done, lo, width)
+        for n, (sent, heard) in enumerate(me.offsets(axes)):
+            sems = (ag_send.at[which, stage, p, n], ag_recv.at[which, stage, p, n])
+            theirs = box(buf, heard, done, lo, width)
+            out.append(
+                (remote(own, own, *sems, me.to(**sent)), remote(theirs, theirs, *sems, me.to(**heard)))
+            )
+        return out
 
     def swap(which, buf):
         out = []
@@ -302,7 +336,10 @@
         return out
 
     student_stages = [gather(1, sb, PARTS_S, s) for s in range(3)]
-    teacher_stages = [gather(0, tb, PARTS_T, s) for s in range(3)]
+    teacher_stages = [[], []]
+    for p, (lo, width, done, first, second) in enumerate(PARTS_T):
+        teacher_stages[0] += one_part(0, tb, 0, p, lo, width, first, done)
+        teacher_stages[1] += one_part(0, tb, 1, p, lo, width, second, done + first)
     student_swap, teacher_swap = swap(1, sb), swap(0, tb)
 
     for k in (1, 2, 3):
@@ -312,51 +349,64 @@
     sb[me.c, me.y, me.z, me.x] = asm_s[...].astype(BF16)
     start_all(student_stages[0])
 
-    own_copy.wait()
-    total = rb[0].astype(F32)
-
-    def add_one(k, acc):
-        frm = lax.rem(tp + 32 - k, 32)
-        a_copy(k, frm).wait_recv()
-        return acc + rb[k].astype(F32)
-
-    total = lax.fori_loop(1, 32, add_one, total)
-
-    def row_total(n, part):
-        mean_out[n] = jnp.broadcast_to(part, (16, LANES))
-        mean_in[n, me.x] = mean_out[n]
-        copies = []
-        for k in (1, 2, 3):
-            to, frm = me.shifted("x", k), me.shifted("x", 4 - k)
-            sems = (x_send.at[2 + n, k - 1], x_recv.at[2 + n, k - 1])
-            copies.append(
-                (
-                    remote(mean_out.at[n], mean_in.at[n, me.x], *sems, me.along("x", to)),
-                    remote(mean_out.at[n], mean_in.at[n, frm], *sems, me.along("x", frm)),
-                )
-            )
-        start_all(copies)
-        return copies
-
-    def row_mean(n, copies):
-        arrive_all(copies)
-        whole = mean_in[n, 0] + mean_in[n, 1] + mean_in[n, 2] + mean_in[n, 3]
-        return whole[:, 0:1] / D_T
-
-    first_mean = row_total(0, jnp.sum(total * total, axis=1, keepdims=True))
+    arrive_all(first_stage)
+    for p, (lo, width, axis, plane) in enumerate(PARTS_A):
+        came = first_in[p]
+        count = came.shape[0]
+
+        @pl.loop(0, came.shape[1] * came.shape[2] * came.shape[3])
+        def _(n, lo=lo, width=width, axis=axis, plane=plane, came=came, count=count):
+            at, slot = {axis: me.at(axis)}, {axis: 0}
+            for a in reversed(plane):
+                size = 2 if a == "h" else 4
+                at[a] = slot[a] = lax.rem(n, size)
+                n = lax.div(n, size)
+            cols = slice(lo, lo + width)
+            whole = pb[at["h"], at["z"], at["x"], :, cols].astype(F32)
+            for i in range(count):
+                whole = whole + came[i, slot["h"], slot["z"], slot["x"]].astype(F32)
+            pb[at["h"], at["z"], at["x"], :, cols] = whole.astype(BF16)
+
+    start_all(second_stage)
     arrive_all(student_stages[0])
     start_all(student_stages[1])
-    for k in (1, 2, 3):
-        x_arrival(1, res_out, res_in, k).wait_recv()
-    for i in range(4):
-        asm_t[4 * i : 4 * i + 4, :] = res_in[i].astype(F32)
-    post = total * lax.rsqrt(row_mean(0, first_mean) + EPS) * post_ref[:, own_cols]
-    final = asm_t[...] + post
-    second_mean = row_total(1, jnp.sum(final * final, axis=1, keepdims=True))
+    arrive_all(residual_copies)
+    for q in range(4):
+        for i in range(4):
+            asm_t[q, 4 * i : 4 * i + 4, :] = res_in[i, :, q * QT : (q + 1) * QT].astype(F32)
+    arrive_all(second_stage)
+    for p, (lo, width, axis, plane) in enumerate(PARTS_A):
+        whole = pb[me.y_hi, me.z, me.x, :, lo : lo + width].astype(F32)
+        for n in range(second_in[p].shape[0]):
+            whole = whole + second_in[p][n].astype(F32)
+        rows_in[me.x, :, lo : lo + width] = whole.astype(BF16)
+
+    row_copies = spread(2, rows_in.at[me.x], lambda i: rows_in.at[i])
+    start_all(row_copies)
     arrive_all(student_stages[1])
     start_all(student_stages[2])
-    normed = final * lax.rsqrt(row_mean(1, second_mean) + EPS) * final_ref[:, own_cols]
-    tb[me.c, me.y, me.z, me.x] = normed.astype(BF16)
+    arrive_all(row_copies)
+
+    def row_inverse(quarters):
+        total = sum(jnp.sum(v * v, axis=1, keepdims=True) for v in quarters)
+        return lax.rsqrt(total / D_T + EPS)
+
+    sums = [rows_in[q].astype(F32) for q in range(4)]
+    scale = row_inverse(sums)
+    for q in range(4):
+        cols = slice(q * QT, (q + 1) * QT)
+        asm_t[q] = asm_t[q] + sums[q] * scale * post_ref[cols].reshape(1, QT)
+    scale = row_inverse([asm_t[q] for q in range(4)])
+    for q in range(4):
+        cols = slice(q * QT, (q + 1) * QT)
+        normed[q] = (asm_t[q] * scale * final_ref[cols].reshape(1, QT)).astype(BF16)
+    for lo, width, done, first, second in PARTS_T:
+        cols = slice(lo, lo + width)
+        if done:
+            for q in range(4):
+                tb[me.c, me.y, me.z, q, :, cols] = normed[q, :, cols]
+        else:
+            tb[me.c, me.y, me.z, me.x, :, cols] = normed[me.x, :, cols]
     start_all(teacher_stages[0])
 
     for n in range(3):
@@ -376,40 +426,37 @@
     start_all(teacher_stages[1])
     arrive_all(student_stages[2])
     start_all(student_swap)
-    arrive_all(teacher_stages[1])
-    start_all(teacher_stages[2])
-
-    def live_rows(buf, q, width):
-        return jnp.concatenate(
-            [
-                buf[:, 0:2, :, q].reshape(256, width),
-                buf[:, 2:4, 0:2, q].reshape(128, width),
-            ],
-            axis=0,
-        )
-
-    def logits(buf, head, out, width):
+
+    def logits(buf, head, out, width, core):
+        rows = pl.ds(pl.multiple_of(core * HALF, HALF), HALF)
+
         @pl.loop(0, VOC // 256)
         def _(n):
             cols = pl.ds(pl.multiple_of(n * 256, 256), 256)
             acc = None
             for q in range(4):
-                term = jnp.dot(
-                    live_rows(buf, q, width),
-                    head[q * width : (q + 1) * width, cols],
-                    preferred_element_type=F32,
+                live = jnp.concatenate(
+                    [
+                        buf[core, 0:2, :, q].reshape(128, width),
+                        buf[core, 2:4, 0:2, q].reshape(64, width),
+                    ],
+                    axis=0,
                 )
+                head_rows = head[q * width : (q + 1) * width, cols]
+                term = jnp.dot(live, head_rows, preferred_element_type=F32)
                 acc = term if acc is None else acc + term
-            out[:, cols] = acc
-
+            out[rows, cols] = acc
+
+    load_s.wait()
+    logits(sb, w_s, s_log, QS, me.c)
     arrive_all(student_swap)
-    load_s.wait()
-    logits(sb, w_s, s_log, QS)
-    arrive_all(teacher_stages[2])
+    logits(sb, w_s, s_log, QS, 1 - me.c)
+    load_t.wait()
+    arrive_all(teacher_stages[1])
     start_all(teacher_swap)
-    load_t.wait()
+    logits(tb, w_t, t_log, QT, me.c)
     arrive_all(teacher_swap)
-    logits(tb, w_t, t_log, QT)
+    logits(tb, w_t, t_log, QT, 1 - me.c)
 
     first_col = (position * VOC).astype(F32)
 
@@ -452,7 +499,6 @@
             label += v[5:6]
         return [t_max, t_sum, cross, s_max, s_sum, label, values[0][6:7]]
 
-    stat_copies = []
     for n, axis in enumerate("cxyz"):
         copies = []
         for k in (1,) if axis == "c" else (1, 2, 3):
@@ -462,7 +508,6 @@
             copy = remote(stat.at[n], dst, *sems, to)
             copies.append((copy, copy))
         start_all(copies)
-        stat_copies += copies
         arrive_all(copies)
         values = [stat[n]] + [stat_in[n, k] for k in range(len(copies))]
         for i, line in enumerate(merged(values)):
@@ -503,8 +548,11 @@
                 (((1,), (1,)), ((), ())),
                 preferred_element_type=F32,
             ).astype(BF16)
-            g[:, 0:2, :, q, :, lo : lo + width] = share[0:256].reshape(2, 2, 4, 16, width)
-            g[:, 2:4, 0:2, q, :, lo : lo + width] = share[256:384].reshape(2, 2, 2, 16, width)
+            cols = slice(lo, lo + width)
+            for c in range(2):
+                own = share[c * HALF : (c + 1) * HALF]
+                g[c, 0:2, :, q, :, cols] = own[0:128].reshape(2, 4, 16, width)
+                g[c, 2:4, 0:2, q, :, cols] = own[128:192].reshape(2, 2, 16, width)
 
     core_copies = []
     for n, (y, z) in enumerate(((pl.ds(0, 2), pl.ds(0, 4)), (pl.ds(2, 2), pl.ds(0, 2)))):
@@ -535,7 +583,7 @@
             for k in (1, 2, 3):
                 to = me.shifted(axis, k)
                 copy = remote(
-                    box(g, axis, to, left, lo, width),
+                    box(g, {axis: to}, left, lo, width),
                     rr[stage][p].at[k - 1],
                     rs_send.at[stage, p, k - 1],
                     rs_recv.at[stage, p, k - 1],
@@ -544,7 +592,6 @@
                 made.append((copy, copy))
         start_all(made)
         arrive_all(made)
-        core_copies += made
         for p, (lo, width, order) in enumerate(PARTS_G):
             left = order[stage + 1 :]
             came = rr[stage][p]
@@ -588,30 +635,27 @@
         x_arrival(4, ng_out, ng_in, k).wait_recv()
     norm_grad = jnp.concatenate([ng_in[q] for q in range(4)], axis=1)
     live = me.y_hi * 4 + me.z < 6
-    scaled = norm_grad * s_gain_ref[...]
+    scaled = norm_grad * s_gain
     inner = jnp.mean(scaled * hidden, axis=1, keepdims=True)
     grad = inverse * scaled - hidden * (inverse * inverse * inverse) * inner
     grad_ref[...] = jnp.where(live, grad, 0.0)
 
-    @pl.loop(1, 32)
-    def _(k):
-        a_copy(k, lax.rem(tp + k, 32)).wait_send()
-
     for k in (1, 2, 3):
         x_copy(0, stu_out, stu_in, k).wait_send()
-        x_copy(1, res_out, res_in, k).wait_send()
         x_copy(4, ng_out, ng_in, k).wait_send()
     for n in range(3):
         tab_copy(n)[0].wait_send()
-    sent_all(first_mean + second_mean)
-    for copies in student_stages + teacher_stages + [student_swap, teacher_swap]:
-        sent_all(copies)
-    sent_all(stat_copies + core_copies)
+    for sent, unused in opened:
+        sent.wait_send()
 
 
 def scratch():
     dma = pltpu.SemaphoreType.DMA
     vm = pltpu.VMEM
+    first = []
+    for lo, width, axis, plane in PARTS_A:
+        spots = [1 if a == axis else 2 if a == "h" else 4 for a in "hzx"]
+        first.append(vm((1 if axis == "h" else 3, *spots, 16, width), BF16))
     rr = []
     for stage in range(3):
         row = []
@@ -622,17 +666,18 @@
     return {
         "w_t": vm((D_T, VOC), BF16),
         "w_s": vm((D_S, VOC), BF16),
-        "rb": vm((32, 16, QT), BF16),
+        "pb": vm((2, 4, 4, 16, QT), BF16),
+        "first_in": tuple(first),
+        "second_in": tuple(vm((n, 16, PARTS_A[0][1]), BF16) for n in (7, 7, 15)),
+        "rows_in": vm((4, 16, QT), BF16),
         "tb": vm((2, 4, 4, 4, 16, QT), BF16),
         "sb": vm((2, 4, 4, 4, 16, QS), BF16),
-        "res_out": vm((4, 4, QT), BF16),
-        "res_in": vm((4, 4, QT), BF16),
+        "res_in": vm((4, 4, D_T), BF16),
         "stu_out": vm((4, 4, QS), BF16),
         "stu_in": vm((4, 4, QS), BF16),
-        "asm_t": vm((16, QT), F32),
+        "asm_t": vm((4, 16, QT), F32),
         "asm_s": vm((16, QS), F32),
-        "mean_out": vm((2, 16, LANES), F32),
-        "mean_in": vm((2, 4, 16, LANES), F32),
+        "normed": vm((4, 16, QT), BF16),
         "tab_own": vm((8, LANES), F32),
         "tab": vm((4, 8, LANES), F32),
         "lab_col": vm((ROWS, LANES), F32),
@@ -650,15 +695,17 @@
         "ng_out": vm((4, 4, QS), F32),
         "ng_in": vm((4, 4, QS), F32),
         "sem_w": dma((2,)),
-        "a_send": dma((32,)),
-        "a_recv": dma((32,)),
-        "a_own": dma(()),
+        "a_own": dma((4,)),
+        "f_send": dma((3, 3)),
+        "f_recv": dma((3, 3)),
+        "h_send": dma((3, 15)),
+        "h_recv": dma((3, 15)),
         "x_send": dma((5, 3)),
         "x_recv": dma((5, 3)),
         "tab_send": dma((3,)),
         "tab_recv": dma((3,)),
-        "ag_send": dma((2, 3, 3, 3)),
-        "ag_recv": dma((2, 3, 3, 3)),
+        "ag_send": dma((2, 3, 3, 15)),
+        "ag_recv": dma((2, 3, 3, 15)),
         "sib_send": dma((3, 2)),
         "sib_recv": dma((3, 2)),
         "st_send": dma((4, 3)),
@@ -715,13 +762,13 @@
         ),
         name="distill",
     )(
-        teacher_partial,
+        teacher_partial.reshape(2, 4, 16, D_T),
         teacher_residual,
-        post_gain.reshape(1, -1),
-        final_gain.reshape(1, -1),
+        post_gain,
+        final_gain,
         teacher_head,
         student_hidden,
-        student_gain.reshape(1, -1),
+        student_gain,
         student_head,
         labels.reshape(1, -1),
         lengths,

time: 123 us -> 111 us (0.902)
  Pallas kernels: 115 us -> 108 us
  local copies, waits for them, and re-layouts: 6.57 us -> 2.56 us
    pallas_call x1, Pallas kernels: 115 us -> 108 us  [shards(): pl.pallas_call(body, out_shape=(jax.ShapeDtypeStruct((4, D_S), F32), jax....]
    reshape x3 -> x0, local copies, waits for them, and re-layouts: 4.02 us -> none  [the longest x1 1.35 us: shards(): final_gain.reshape(1, -1)]
where the time goes in v2:
time: 111 us
  Pallas kernels  108 us (97%)
  local copies, waits for them, and re-layouts  2.56 us (2%)
    pallas_call x1, Pallas kernels, shards(): pl.pallas_call(body, out_shape=(jax.ShapeDtypeStruct((4, D_S), F32), jax....  108 us

profile of v2, /device:TPU:0, one launch (start us, length us, event | category | flops | bytes accessed | tf_op | source)
XLA Modules:
  0.0 110.9 jit_solution(4114443431490380233)
XLA Ops:
  0.6 107.7 %distill.1 = (f32[4,3584]{1,0:T(4,128)}, f32[1,128]{1,0:T(1,128)}) custom-call(bf16[2,4,16,4608]{3,2,1,0:T(8,128)(2,1)} %bitcast.4, bf16[4,4608]{1,0:T(4,128)(2,1)} %refs_1_.1, f32[4608]{0:T(1024)} %refs_2_.1, f32[4608]{0:T(1024)} %refs_3_.1, bf16[4608,1024]{1,0:T(8,128)(2,1)} %refs_4_.1, bf16[4,3584]{1,0:T(4,128)(2,1)} %refs_5_.1, f32[3584]{0:T(1024)} %refs_6_.1, ...), custom_call_target="tpu_custom_call" | custom-call | tf_op jit(solution)/shard_map/distill/pallas_call | solution.py:740
  108.4 1.1 %slice_bitcast_fusion = f32[4]{0:T(128)} fusion(f32[1,128]{1,0:T(1,128)} %get-tuple-element.5), kind=kLoop, calls=%fused_computation | loop fusion | bytes 32 | tf_op jit(solution)/shard_map/squeeze | solution.py:776
  109.5 1.4 %copy.13 = f32[4,3584]{1,0:T(4,128)} copy(f32[4,3584]{1,0:T(4,128)} %get-tuple-element.8) | data formatting | bytes 114688

commit v3 on v2

--- a/solution.py
+++ b/solution.py
@@ -34,7 +34,9 @@
 PARTS_A = ((0, 384, "x", "hz"), (384, 384, "z", "hx"), (768, 384, "h", "zx"))
 PARTS_T = ((0, 384, "x", "y", "z"), (384, 384, "x", "z", "y"), (768, 384, "", "yz", "x"))
 PARTS_S = ((0, 256, "xyz"), (256, 384, "yzx"), (640, 256, "zxy"))
-PARTS_G = ((0, 256, "zyx"), (256, 384, "xzy"), (640, 256, "yxz"))
+PARTS_G = ((0, 256, "z", "y"), (256, 256, "y", "z"))
+LO_X, W_X = (512, 384)
+W_YZ = 512
 
 
 def live_pieces():
@@ -46,6 +48,7 @@
 
 
 PIECES = live_pieces()
+LIVE = ((pl.ds(0, 2), pl.ds(0, 4)), (pl.ds(2, 2), pl.ds(0, 2)))
 
 
 class Place:
@@ -131,7 +134,10 @@
     loss_blk,
     g,
     core_in,
-    rr,
+    rr0,
+    rr_x,
+    rr1,
+    rr2,
     ng_out,
     ng_in,
     sem_w,
@@ -150,8 +156,16 @@
     sib_recv,
     st_send,
     st_recv,
+    cs_send,
+    cs_recv,
     rs_send,
     rs_recv,
+    rx_send,
+    rx_recv,
+    r1_send,
+    r1_recv,
+    r2_send,
+    r2_recv,
 ):
     me = Place()
     tp = me.y_hi * 16 + me.z * 4 + me.x
@@ -160,9 +174,6 @@
 
     load_s = pltpu.make_async_copy(s_head_ref, w_s, sem_w.at[0])
     load_t = pltpu.make_async_copy(t_head_ref, w_t, sem_w.at[1])
-    load_s.start()
-    load_t.start()
-
     own_copies = []
     for q in range(4):
         copy = pltpu.make_async_copy(
@@ -219,6 +230,10 @@
             )
             second_stage.append((copy, copy))
 
+    start_all(first_stage)
+    load_t.start()
+    load_s.start()
+
     hidden = hidden_ref[...].astype(F32)
     s_gain = s_gain_ref[...].reshape(1, D_S)
     inverse = lax.rsqrt(jnp.mean(hidden * hidden, axis=-1, keepdims=True) + EPS)
@@ -250,8 +265,6 @@
 
     for k in (1, 2, 3):
         x_copy(0, stu_out, stu_in, k).start()
-    start_all(first_stage)
-
     def spread(kind, own, where):
         copies = []
         for k in (1, 2, 3):
@@ -316,18 +329,29 @@
 
     def one_part(which, buf, stage, p, lo, width, axes, done):
         out = []
-        own = box(buf, {}, done, lo, width)
+        cols = pl.ds(lo, width)
         for n, (sent, heard) in enumerate(me.offsets(axes)):
-            sems = (ag_send.at[which, stage, p, n], ag_recv.at[which, stage, p, n])
-            theirs = box(buf, heard, done, lo, width)
-            out.append(
-                (remote(own, own, *sems, me.to(**sent)), remote(theirs, theirs, *sems, me.to(**heard)))
-            )
+            if "y" in done and "z" in done:
+                boxes = [
+                    (buf.at[me.c, y, z, pl.ds(me.x, 1), :, cols], buf.at[me.c, y, z, pl.ds(heard["x"], 1), :, cols])
+                    for y, z in LIVE
+                ]
+            else:
+                boxes = [(box(buf, {}, done, lo, width), box(buf, heard, done, lo, width))]
+            for i, (own, theirs) in enumerate(boxes):
+                at = n * len(boxes) + i
+                sems = (ag_send.at[which, stage, p, at], ag_recv.at[which, stage, p, at])
+                out.append(
+                    (
+                        remote(own, own, *sems, me.to(**sent)),
+                        remote(theirs, theirs, *sems, me.to(**heard)),
+                    )
+                )
         return out
 
     def swap(which, buf):
         out = []
-        for n, (y, z) in enumerate(((pl.ds(0, 2), pl.ds(0, 4)), (pl.ds(2, 2), pl.ds(0, 2)))):
+        for n, (y, z) in enumerate(LIVE):
             sems = (sib_send.at[which, n], sib_recv.at[which, n])
             own, theirs = buf.at[me.c, y, z], buf.at[1 - me.c, y, z]
             out.append(
@@ -383,8 +407,6 @@
 
     row_copies = spread(2, rows_in.at[me.x], lambda i: rows_in.at[i])
     start_all(row_copies)
-    arrive_all(student_stages[1])
-    start_all(student_stages[2])
     arrive_all(row_copies)
 
     def row_inverse(quarters):
@@ -422,10 +444,10 @@
     g[:, 2:4, 2:4] = jnp.zeros((2, 2, 2, 4, 16, QS), BF16)
     loss_blk[:, 2:4, 2:4] = jnp.zeros((2, 2, 2, 16, LANES), F32)
 
+    arrive_all(student_stages[1])
     arrive_all(teacher_stages[0])
     start_all(teacher_stages[1])
-    arrive_all(student_stages[2])
-    start_all(student_swap)
+    start_all(student_stages[2])
 
     def logits(buf, head, out, width, core):
         rows = pl.ds(pl.multiple_of(core * HALF, HALF), HALF)
@@ -447,16 +469,18 @@
                 acc = term if acc is None else acc + term
             out[rows, cols] = acc
 
+    load_t.wait()
+    arrive_all(teacher_stages[1])
+    start_all(teacher_swap)
+    logits(tb, w_t, t_log, QT, me.c)
+    arrive_all(student_stages[2])
+    start_all(student_swap)
+    arrive_all(teacher_swap)
+    logits(tb, w_t, t_log, QT, 1 - me.c)
     load_s.wait()
     logits(sb, w_s, s_log, QS, me.c)
     arrive_all(student_swap)
     logits(sb, w_s, s_log, QS, 1 - me.c)
-    load_t.wait()
-    arrive_all(teacher_stages[1])
-    start_all(teacher_swap)
-    logits(tb, w_t, t_log, QT, me.c)
-    arrive_all(teacher_swap)
-    logits(tb, w_t, t_log, QT, 1 - me.c)
 
     first_col = (position * VOC).astype(F32)
 
@@ -539,84 +563,133 @@
         scale = LOSS_SCALE * wgt_col[rows, 0:1]
         lg[rows, :] = (scale * ((1.0 + BETA) * s_prob - t_prob - BETA * hit)).astype(BF16)
 
-    for q in range(4):
-        for lo in range(0, QS, 128 * 7):
-            width = min(128 * 7, QS - lo)
-            share = lax.dot_general(
-                lg[...],
-                w_s[q * QS + lo : q * QS + lo + width, :],
-                (((1,), (1,)), ((), ())),
-                preferred_element_type=F32,
-            ).astype(BF16)
-            cols = slice(lo, lo + width)
-            for c in range(2):
-                own = share[c * HALF : (c + 1) * HALF]
-                g[c, 0:2, :, q, :, cols] = own[0:128].reshape(2, 4, 16, width)
-                g[c, 2:4, 0:2, q, :, cols] = own[128:192].reshape(2, 2, 16, width)
-
-    core_copies = []
-    for n, (y, z) in enumerate(((pl.ds(0, 2), pl.ds(0, 4)), (pl.ds(2, 2), pl.ds(0, 2)))):
-        copy = remote(
-            g.at[1 - me.c, y, z],
-            core_in.at[y, z],
-            sib_send.at[2, n],
-            sib_recv.at[2, n],
-            me.sibling(),
+    def quarter(k, core):
+        q = me.shifted("x", k)
+        return lax.dot_general(
+            lg[pl.ds(pl.multiple_of(core * HALF, HALF), HALF), :],
+            w_s[pl.ds(pl.multiple_of(q * QS, QS), QS), :],
+            (((1,), (1,)), ((), ())),
+            preferred_element_type=F32,
         )
-        core_copies.append((copy, copy))
-    start_all(core_copies)
-    arrive_all(core_copies)
+
+    def first_reduce(k):
+        q = me.shifted("x", k)
+        copies = []
+        for p, (lo, width, axis, then) in enumerate(PARTS_G):
+            for n, (sent, heard) in enumerate(me.offsets(axis)):
+                where = {a: pl.ds(sent[a], 1) if a in sent else slice(None) for a in "yz"}
+                copy = remote(
+                    g.at[me.c, where["y"], where["z"], q, :, pl.ds(lo, width)],
+                    rr0[p].at[n, k - 1],
+                    rs_send.at[p, n, k - 1],
+                    rs_recv.at[p, n, k - 1],
+                    me.to(**sent),
+                )
+                copies.append((copy, copy))
+        if k < 4:
+            for i, (y, z) in enumerate(LIVE):
+                copy = remote(
+                    g.at[me.c, y, z, q, :, pl.ds(LO_X, W_X)],
+                    rr_x.at[k - 1, y, z],
+                    rx_send.at[k - 1, i],
+                    rx_recv.at[k - 1, i],
+                    me.along("x", q),
+                )
+                copies.append((copy, copy))
+        return copies
+
+    core_copies, reduce_copies = [], []
+    for k in range(1, 6):
+        if k < 5:
+            q = me.shifted("x", k)
+            share = quarter(k, 1 - me.c).astype(BF16)
+            g[1 - me.c, 0:2, :, q] = share[0:128].reshape(2, 4, 16, QS)
+            g[1 - me.c, 2:4, 0:2, q] = share[128:192].reshape(2, 2, 16, QS)
+            copies = []
+            for i, (y, z) in enumerate(LIVE):
+                copy = remote(
+                    g.at[1 - me.c, y, z, q],
+                    core_in.at[k - 1, y, z],
+                    cs_send.at[k - 1, i],
+                    cs_recv.at[k - 1, i],
+                    me.sibling(),
+                )
+                copies.append((copy, copy))
+            start_all(copies)
+            core_copies.append(copies)
+        if k > 1:
+            q = me.shifted("x", k - 1)
+            share = quarter(k - 1, me.c)
+            arrive_all(core_copies[k - 2])
+            other = core_in[k - 2, 0:2].reshape(128, QS).astype(F32)
+            g[me.c, 0:2, :, q] = (share[0:128] + other).astype(BF16).reshape(2, 4, 16, QS)
+            other = core_in[k - 2, 2:4, 0:2].reshape(64, QS).astype(F32)
+            g[me.c, 2:4, 0:2, q] = (share[128:192] + other).astype(BF16).reshape(2, 2, 16, QS)
+            copies = first_reduce(k - 1)
+            start_all(copies)
+            reduce_copies += copies
+
+    arrive_all(reduce_copies)
+    for p, (lo, width, axis, then) in enumerate(PARTS_G):
+        cols = slice(lo, lo + width)
+        for k in range(1, 5):
+            q = me.shifted("x", k)
+
+            @pl.loop(0, 4)
+            def _(i, p=p, axis=axis, then=then, cols=cols, k=k, q=q):
+                at = {axis: me.at(axis), then: i}
+                slot = {axis: 0, then: i}
+                whole = g[me.c, at["y"], at["z"], q, :, cols].astype(F32)
+                for n in range(3):
+                    whole = whole + rr0[p][n, k - 1, slot["y"], slot["z"]].astype(F32)
+                g[me.c, at["y"], at["z"], q, :, cols] = whole.astype(BF16)
+
+    cols_x = slice(LO_X, LO_X + W_X)
     for ys, zs in (((0, 1), 4), ((2, 3), 2)):
         for y in ys:
 
-            @pl.loop(0, zs * 4)
-            def _(i, y=y):
-                z, x = lax.div(i, 4), lax.rem(i, 4)
-                both = g[me.c, y, z, x].astype(F32) + core_in[y, z, x].astype(F32)
-                g[me.c, y, z, x] = both.astype(BF16)
-
-    totals = []
-    for stage in range(3):
-        made = []
-        for p, (lo, width, order) in enumerate(PARTS_G):
-            axis, left = order[stage], order[stage + 1 :]
-            for k in (1, 2, 3):
-                to = me.shifted(axis, k)
-                copy = remote(
-                    box(g, {axis: to}, left, lo, width),
-                    rr[stage][p].at[k - 1],
-                    rs_send.at[stage, p, k - 1],
-                    rs_recv.at[stage, p, k - 1],
-                    me.along(axis, to),
-                )
-                made.append((copy, copy))
-        start_all(made)
-        arrive_all(made)
-        for p, (lo, width, order) in enumerate(PARTS_G):
-            left = order[stage + 1 :]
-            came = rr[stage][p]
-
-            def summed(y, z, x, i, j, k):
-                whole = g[me.c, y, z, x, :, lo : lo + width].astype(F32)
+            @pl.loop(0, zs)
+            def _(z, y=y):
+                whole = g[me.c, y, z, me.x, :, cols_x].astype(F32)
                 for n in range(3):
-                    whole = whole + came[n, i, j, k].astype(F32)
-                return whole
-
-            if stage == 2:
-                whole = summed(me.y, me.z, me.x, 0, 0, 0)
-                for i in range(4):
-                    ng_out[i, :, lo : lo + width] = whole[4 * i : 4 * i + 4]
-            else:
-
-                @pl.loop(0, 4 ** len(left))
-                def _(n, left=left, lo=lo, width=width, summed=summed):
-                    at = {a: me.at(a) for a in "yzx"}
-                    slot = {a: 0 for a in "yzx"}
-                    for a in left:
-                        at[a] = slot[a] = lax.rem(n, 4)
-                        n = lax.div(n, 4)
-                    whole = summed(at["y"], at["z"], at["x"], slot["y"], slot["z"], slot["x"])
-                    g[me.c, at["y"], at["z"], at["x"], :, lo : lo + width] = whole.astype(BF16)
+                    whole = whole + rr_x[n, y, z].astype(F32)
+                g[me.c, y, z, me.x, :, cols_x] = whole.astype(BF16)
+
+    second = []
+    for p, (lo, width, axis, then) in enumerate(PARTS_G):
+        for n, (sent, heard) in enumerate(me.offsets(then)):
+            at = {axis: me.at(axis), **sent}
+            copy = remote(
+                g.at[me.c, at["y"], at["z"], :, :, pl.ds(lo, width)],
+                rr1.at[p, n],
+                r1_send.at[p, n],
+                r1_recv.at[p, n],
+                me.to(**sent),
+            )
+            second.append((copy, copy))
+    for n, (sent, heard) in enumerate(me.offsets("yz")):
+        copy = remote(
+            g.at[me.c, sent["y"], sent["z"], me.x, :, pl.ds(LO_X, W_X)],
+            rr2.at[n],
+            r2_send.at[n],
+            r2_recv.at[n],
+            me.to(**sent),
+        )
+        second.append((copy, copy))
+    start_all(second)
+    arrive_all(second)
+    for p, (lo, width, axis, then) in enumerate(PARTS_G):
+        for q in range(4):
+            whole = g[me.c, me.y, me.z, q, :, lo : lo + width].astype(F32)
+            for n in range(3):
+                whole = whole + rr1[p, n, q].astype(F32)
+            for i in range(4):
+                ng_out[i, :, q * W_YZ + lo : q * W_YZ + lo + width] = whole[4 * i : 4 * i + 4]
+    whole = g[me.c, me.y, me.z, me.x, :, cols_x].astype(F32)
+    for n in range(15):
+        whole = whole + rr2[n].astype(F32)
+    for i in range(4):
+        ng_out[i, :, 4 * W_YZ : 4 * W_YZ + W_X] = whole[4 * i : 4 * i + 4]
 
     ng_in[me.x] = ng_out[me.x]
     for k in (1, 2, 3):
@@ -633,7 +706,12 @@
 
     for k in (1, 2, 3):
         x_arrival(4, ng_out, ng_in, k).wait_recv()
-    norm_grad = jnp.concatenate([ng_in[q] for q in range(4)], axis=1)
+    norm_parts = []
+    for q in range(4):
+        cols = slice(q * W_YZ, (q + 1) * W_YZ)
+        norm_parts.append(ng_in[0, :, cols] + ng_in[1, :, cols] + ng_in[2, :, cols] + ng_in[3, :, cols])
+        norm_parts.append(ng_in[q, :, 4 * W_YZ : 4 * W_YZ + W_X])
+    norm_grad = jnp.concatenate(norm_parts, axis=1)
     live = me.y_hi * 4 + me.z < 6
     scaled = norm_grad * s_gain
     inner = jnp.mean(scaled * hidden, axis=1, keepdims=True)
@@ -656,13 +734,10 @@
     for lo, width, axis, plane in PARTS_A:
         spots = [1 if a == axis else 2 if a == "h" else 4 for a in "hzx"]
         first.append(vm((1 if axis == "h" else 3, *spots, 16, width), BF16))
-    rr = []
-    for stage in range(3):
-        row = []
-        for lo, width, order in PARTS_G:
-            spots = [4 if a in order[stage + 1 :] else 1 for a in "yzx"]
-            row.append(vm((3, *spots, 16, width), BF16))
-        rr.append(tuple(row))
+    rr0 = []
+    for lo, width, axis, then in PARTS_G:
+        spots = [1 if a == axis else 4 for a in "yz"]
+        rr0.append(vm((3, 4, *spots, 16, width), BF16))
     return {
         "w_t": vm((D_T, VOC), BF16),
         "w_s": vm((D_S, VOC), BF16),
@@ -691,9 +766,12 @@
         "loss_blk": vm((2, 4, 4, 16, LANES), F32),
         "g": vm((2, 4, 4, 4, 16, QS), BF16),
         "core_in": vm((4, 4, 4, 16, QS), BF16),
-        "rr": tuple(rr),
-        "ng_out": vm((4, 4, QS), F32),
-        "ng_in": vm((4, 4, QS), F32),
+        "rr0": tuple(rr0),
+        "rr_x": vm((3, 4, 4, 16, W_X), BF16),
+        "rr1": vm((2, 3, 4, 16, PARTS_G[0][1]), BF16),
+        "rr2": vm((15, 16, W_X), BF16),
+        "ng_out": vm((4, 4, 4 * W_YZ + W_X), F32),
+        "ng_in": vm((4, 4, 4 * W_YZ + W_X), F32),
         "sem_w": dma((2,)),
         "a_own": dma((4,)),
         "f_send": dma((3, 3)),
@@ -710,8 +788,16 @@
         "sib_recv": dma((3, 2)),
         "st_send": dma((4, 3)),
         "st_recv": dma((4, 3)),
-        "rs_send": dma((3, 3, 3)),
-        "rs_recv": dma((3, 3, 3)),
+        "cs_send": dma((4, 2)),
+        "cs_recv": dma((4, 2)),
+        "rs_send": dma((2, 3, 4)),
+        "rs_recv": dma((2, 3, 4)),
+        "rx_send": dma((3, 2)),
+        "rx_recv": dma((3, 2)),
+        "r1_send": dma((2, 3)),
+        "r1_recv": dma((2, 3)),
+        "r2_send": dma((15,)),
+        "r2_recv": dma((15,)),
     }
 
 

time: 111 us -> 109 us (0.982)
  Pallas kernels: 108 us -> 106 us
    pallas_call x1, Pallas kernels: 108 us -> 106 us  [shards(): pl.pallas_call(body, out_shape=(jax.ShapeDtypeStruct((4, D_S), F32), jax....]
where the time goes in v3:
time: 109 us
  Pallas kernels  106 us (97%)
  local copies, waits for them, and re-layouts  2.56 us (2%)
    pallas_call x1, Pallas kernels, shards(): pl.pallas_call(body, out_shape=(jax.ShapeDtypeStruct((4, D_S), F32), jax....  106 us

profile of v3, /device:TPU:0, one launch (start us, length us, event | category | flops | bytes accessed | tf_op | source)
XLA Modules:
  0.0 109.3 jit_solution(8354997538193588772)
XLA Ops:
  0.6 106.1 %distill.1 = (f32[4,3584]{1,0:T(4,128)}, f32[1,128]{1,0:T(1,128)}) custom-call(bf16[2,4,16,4608]{3,2,1,0:T(8,128)(2,1)} %bitcast.4, bf16[4,4608]{1,0:T(4,128)(2,1)} %refs_1_.1, f32[4608]{0:T(1024)} %refs_2_.1, f32[4608]{0:T(1024)} %refs_3_.1, bf16[4608,1024]{1,0:T(8,128)(2,1)} %refs_4_.1, bf16[4,3584]{1,0:T(4,128)(2,1)} %refs_5_.1, f32[3584]{0:T(1024)} %refs_6_.1, ...), custom_call_target="tpu_custom_call" | custom-call | tf_op jit(solution)/shard_map/distill/pallas_call | solution.py:826
  106.7 1.1 %slice_bitcast_fusion = f32[4]{0:T(128)} fusion(f32[1,128]{1,0:T(1,128)} %get-tuple-element.5), kind=kLoop, calls=%fused_computation | loop fusion | bytes 32 | tf_op jit(solution)/shard_map/squeeze | solution.py:862
  107.8 1.4 %copy.13 = f32[4,3584]{1,0:T(4,128)} copy(f32[4,3584]{1,0:T(4,128)} %get-tuple-element.8) | data formatting | bytes 114688

commit v4 on v3

--- a/solution.py
+++ b/solution.py
@@ -1,5 +1,6 @@
 import functools
 import itertools
+import types
 
 import jax
 import jax.numpy as jnp
@@ -37,6 +38,7 @@
 PARTS_G = ((0, 256, "z", "y"), (256, 256, "y", "z"))
 LO_X, W_X = (512, 384)
 W_YZ = 512
+GROUPS = 40
 
 
 def live_pieces():
@@ -96,17 +98,28 @@
 
 def kernel(
     partial_ref,
+    residual_hbm,
+    post_hbm,
+    final_hbm,
+    t_head_ref,
+    hidden_hbm,
+    s_gain_hbm,
+    s_head_ref,
+    labels_hbm,
+    lengths_hbm,
+    grad_hbm,
+    loss_hbm,
     residual_ref,
     post_ref,
     final_ref,
-    t_head_ref,
     hidden_ref,
     s_gain_ref,
-    s_head_ref,
     labels_ref,
     lengths_ref,
     grad_ref,
     loss_ref,
+    in_sem,
+    out_sem,
     w_t,
     w_s,
     pb,
@@ -133,6 +146,7 @@
     back,
     loss_blk,
     g,
+    share,
     core_in,
     rr0,
     rr_x,
@@ -142,30 +156,7 @@
     ng_in,
     sem_w,
     a_own,
-    f_send,
-    f_recv,
-    h_send,
-    h_recv,
-    x_send,
-    x_recv,
-    tab_send,
-    tab_recv,
-    ag_send,
-    ag_recv,
-    sib_send,
-    sib_recv,
-    st_send,
-    st_recv,
-    cs_send,
-    cs_recv,
-    rs_send,
-    rs_recv,
-    rx_send,
-    rx_recv,
-    r1_send,
-    r1_recv,
-    r2_send,
-    r2_recv,
+    pool,
 ):
     me = Place()
     tp = me.y_hi * 16 + me.z * 4 + me.x
@@ -174,6 +165,21 @@
 
     load_s = pltpu.make_async_copy(s_head_ref, w_s, sem_w.at[0])
     load_t = pltpu.make_async_copy(t_head_ref, w_t, sem_w.at[1])
+    small_copies = []
+    for n, (src, dst) in enumerate(
+        (
+            (hidden_hbm, hidden_ref),
+            (s_gain_hbm, s_gain_ref),
+            (residual_hbm, residual_ref),
+            (labels_hbm, labels_ref),
+            (lengths_hbm, lengths_ref),
+            (post_hbm, post_ref),
+            (final_hbm, final_ref),
+        )
+    ):
+        copy = pltpu.make_async_copy(src, dst, in_sem.at[n])
+        copy.start()
+        small_copies.append(copy)
     own_copies = []
     for q in range(4):
         copy = pltpu.make_async_copy(
@@ -195,14 +201,30 @@
 
     opened = []
 
-    def start_all(copies):
-        for sent, unused in copies:
-            sent.start()
-        opened.extend(copies)
-
-    def arrive_all(copies):
-        for unused, arrived in copies:
-            arrived.wait_recv()
+    def group(whole):
+        n = len(opened)
+        made = types.SimpleNamespace(
+            whole=whole, send=pool.at[2 * n], recv=pool.at[2 * n + 1], copies=[], started=0
+        )
+        opened.append(made)
+        return made
+
+    def put(made, src, dst, to):
+        made.to = to
+        made.copies.append(remote(src, dst, made.send, made.recv, to))
+
+    def start_all(groups):
+        for made in groups:
+            for copy in made.copies[made.started :]:
+                copy.start()
+            made.started = len(made.copies)
+
+    def both_ends(made):
+        return remote(made.whole, made.whole, made.send, made.recv, made.to)
+
+    def arrive_all(groups):
+        for made in groups:
+            both_ends(made).wait_recv()
 
     for copy in own_copies:
         copy.wait()
@@ -213,26 +235,23 @@
 
     first_stage, second_stage = [], []
     for p, (lo, width, axis, plane) in enumerate(PARTS_A):
+        first = group(first_in[p])
         for n, (sent, heard) in enumerate(me.offsets(axis)):
-            copy = remote(
-                pb_box(sent, lo, width),
-                first_in[p].at[n],
-                f_send.at[p, n],
-                f_recv.at[p, n],
-                me.to(**sent),
-            )
-            first_stage.append((copy, copy))
+            put(first, pb_box(sent, lo, width), first_in[p].at[n], me.to(**sent))
+        second = group(second_in[p])
         for n, (sent, heard) in enumerate(me.offsets(plane)):
             spots = {axis: me.at(axis), **sent}
             src = pb.at[spots["h"], spots["z"], spots["x"], :, pl.ds(lo, width)]
-            copy = remote(
-                src, second_in[p].at[n], h_send.at[p, n], h_recv.at[p, n], me.to(**sent)
-            )
-            second_stage.append((copy, copy))
+            put(second, src, second_in[p].at[n], me.to(**sent))
+        first_stage.append(first)
+        second_stage.append(second)
 
     start_all(first_stage)
     load_t.start()
     load_s.start()
+
+    for copy in small_copies:
+        copy.wait()
 
     hidden = hidden_ref[...].astype(F32)
     s_gain = s_gain_ref[...].reshape(1, D_S)
@@ -243,42 +262,15 @@
     stu_in[me.x] = stu_out[me.x]
     res_in[me.x] = residual_ref[...]
 
-    def x_copy(kind, src, dst, k):
-        to = me.shifted("x", k)
-        return remote(
-            src.at[to],
-            dst.at[me.x],
-            x_send.at[kind, k - 1],
-            x_recv.at[kind, k - 1],
-            me.along("x", to),
-        )
-
-    def x_arrival(kind, src, dst, k):
-        frm = me.shifted("x", 4 - k)
-        return remote(
-            src.at[frm],
-            dst.at[frm],
-            x_send.at[kind, k - 1],
-            x_recv.at[kind, k - 1],
-            me.along("x", frm),
-        )
-
-    for k in (1, 2, 3):
-        x_copy(0, stu_out, stu_in, k).start()
-    def spread(kind, own, where):
-        copies = []
-        for k in (1, 2, 3):
-            frm = me.shifted("x", 4 - k)
-            sems = (x_send.at[kind, k - 1], x_recv.at[kind, k - 1])
-            copies.append(
-                (
-                    remote(own, where(me.x), *sems, me.along("x", me.shifted("x", k))),
-                    remote(own, where(frm), *sems, me.along("x", frm)),
-                )
-            )
-        return copies
-
-    residual_copies = spread(1, residual_ref, lambda i: res_in.at[i])
+    def along_x(whole, src, dst):
+        made = group(whole)
+        for sent, heard in me.offsets("x"):
+            put(made, src(sent["x"]), dst, me.to(**sent))
+        return [made]
+
+    student_copies = along_x(stu_in.at[pl.ds(0, 3)], lambda to: stu_out.at[to], stu_in.at[me.x])
+    start_all(student_copies)
+    residual_copies = along_x(res_in.at[pl.ds(0, 3)], lambda to: residual_ref, res_in.at[me.x])
     start_all(residual_copies)
 
     lane = lax.broadcasted_iota(jnp.int32, (1, LANES), 1)
@@ -288,8 +280,8 @@
         length = lengths_ref[0, i]
         end = start + length
         inside = (lane >= start) & (lane < end)
-        share = 1.0 / jnp.full((1, LANES), length, jnp.int32).astype(F32)
-        weight = jnp.where(inside, share, weight)
+        one_over = 1.0 / jnp.full((1, LANES), length, jnp.int32).astype(F32)
+        weight = jnp.where(inside, one_over, weight)
         start = end
     sub = lax.broadcasted_iota(jnp.int32, (8, LANES), 0)
     label_row = labels_ref[...].astype(F32)
@@ -299,20 +291,10 @@
         jnp.where(sub == 1, jnp.broadcast_to(weight, (8, LANES)), 0.0),
     )
     tab[dp] = tab_own[...]
-    dp_peers = ((0, 1), (1, 0), (1, 1))
-
-    def tab_copy(n):
-        dy, dc = dp_peers[n]
-        y_lo = 1 - me.y_lo if dy else me.y_lo
-        c = 1 - me.c if dc else me.c
-        to = (y_lo, c, me.y_hi, me.z, me.x)
-        return (
-            remote(tab_own, tab.at[dp], tab_send.at[n], tab_recv.at[n], to),
-            remote(tab_own, tab.at[y_lo * 2 + c], tab_send.at[n], tab_recv.at[n], to),
-        )
-
-    for n in range(3):
-        tab_copy(n)[0].start()
+    tables = group(tab.at[pl.ds(0, 3)])
+    for y_lo, c in ((me.y_lo, 1 - me.c), (1 - me.y_lo, me.c), (1 - me.y_lo, 1 - me.c)):
+        put(tables, tab_own, tab.at[dp], (y_lo, c, me.y_hi, me.z, me.x))
+    start_all([tables])
 
     def box(buf, spots, done, lo, width):
         where = []
@@ -320,58 +302,37 @@
             where.append(pl.ds(0, 4) if a in done else pl.ds(spots.get(a, me.at(a)), 1))
         return buf.at[me.c, where[0], where[1], where[2], :, pl.ds(lo, width)]
 
-    def gather(which, buf, parts, stage):
-        out = []
-        for p, (lo, width, order) in enumerate(parts):
-            axis, done = order[stage], order[:stage]
-            out += one_part(which, buf, stage, p, lo, width, axis, done)
-        return out
-
-    def one_part(which, buf, stage, p, lo, width, axes, done):
-        out = []
+    def one_part(buf, lo, width, axes, done, whole=None):
         cols = pl.ds(lo, width)
-        for n, (sent, heard) in enumerate(me.offsets(axes)):
-            if "y" in done and "z" in done:
-                boxes = [
-                    (buf.at[me.c, y, z, pl.ds(me.x, 1), :, cols], buf.at[me.c, y, z, pl.ds(heard["x"], 1), :, cols])
-                    for y, z in LIVE
-                ]
-            else:
-                boxes = [(box(buf, {}, done, lo, width), box(buf, heard, done, lo, width))]
-            for i, (own, theirs) in enumerate(boxes):
-                at = n * len(boxes) + i
-                sems = (ag_send.at[which, stage, p, at], ag_recv.at[which, stage, p, at])
-                out.append(
-                    (
-                        remote(own, own, *sems, me.to(**sent)),
-                        remote(theirs, theirs, *sems, me.to(**heard)),
-                    )
-                )
-        return out
-
-    def swap(which, buf):
-        out = []
-        for n, (y, z) in enumerate(LIVE):
-            sems = (sib_send.at[which, n], sib_recv.at[which, n])
-            own, theirs = buf.at[me.c, y, z], buf.at[1 - me.c, y, z]
-            out.append(
-                (remote(own, own, *sems, me.sibling()), remote(theirs, theirs, *sems, me.sibling()))
-            )
-        return out
-
-    student_stages = [gather(1, sb, PARTS_S, s) for s in range(3)]
-    teacher_stages = [[], []]
-    for p, (lo, width, done, first, second) in enumerate(PARTS_T):
-        teacher_stages[0] += one_part(0, tb, 0, p, lo, width, first, done)
-        teacher_stages[1] += one_part(0, tb, 1, p, lo, width, second, done + first)
-    student_swap, teacher_swap = swap(1, sb), swap(0, tb)
-
-    for k in (1, 2, 3):
-        x_arrival(0, stu_out, stu_in, k).wait_recv()
-    for i in range(4):
-        asm_s[4 * i : 4 * i + 4, :] = stu_in[i].astype(F32)
-    sb[me.c, me.y, me.z, me.x] = asm_s[...].astype(BF16)
-    start_all(student_stages[0])
+        three = [pl.ds(0, 4) if a in done else pl.ds(me.at(a), 1) for a in "yzx"]
+        three["yzx".index(axes[0])] = pl.ds(0, 3)
+        live = LIVE if "y" in done and "z" in done else ()
+        if live:
+            three = [pl.ds(0, 4), pl.ds(0, 3), pl.ds(0, 3)]
+        made = group(buf.at[me.c, three[0], three[1], three[2], :, cols] if whole is None else whole)
+        own = [buf.at[me.c, y, z, pl.ds(me.x, 1), :, cols] for y, z in live]
+        for sent, heard in me.offsets(axes):
+            for src in own or [box(buf, {}, done, lo, width)]:
+                put(made, src, src, me.to(**sent))
+        return made
+
+    def swap(buf):
+        made = group(buf.at[0, pl.ds(0, 3)])
+        for y, z in LIVE:
+            own = buf.at[me.c, y, z]
+            put(made, own, own, me.sibling())
+        return [made]
+
+    student_stages, teacher_stages = [[], [], []], [[], []]
+    for stage in range(3):
+        for lo, width, order in PARTS_S:
+            made = one_part(sb, lo, width, order[stage], order[:stage])
+            student_stages[stage].append(made)
+    for lo, width, done, first, second in PARTS_T:
+        whole = second_in[2] if len(first) == 2 else None
+        teacher_stages[0].append(one_part(tb, lo, width, first, done, whole))
+        teacher_stages[1].append(one_part(tb, lo, width, second, done + first))
+    student_swap, teacher_swap = swap(sb), swap(tb)
 
     arrive_all(first_stage)
     for p, (lo, width, axis, plane) in enumerate(PARTS_A):
@@ -392,8 +353,12 @@
             pb[at["h"], at["z"], at["x"], :, cols] = whole.astype(BF16)
 
     start_all(second_stage)
-    arrive_all(student_stages[0])
-    start_all(student_stages[1])
+    arrive_all(student_copies)
+    for i in range(4):
+        asm_s[4 * i : 4 * i + 4, :] = stu_in[i].astype(F32)
+    sb[me.c, me.y, me.z, me.x] = asm_s[...].astype(BF16)
+    start_all(student_stages[0])
+
     arrive_all(residual_copies)
     for q in range(4):
         for i in range(4):
@@ -405,8 +370,10 @@
             whole = whole + second_in[p][n].astype(F32)
         rows_in[me.x, :, lo : lo + width] = whole.astype(BF16)
 
-    row_copies = spread(2, rows_in.at[me.x], lambda i: rows_in.at[i])
+    row_copies = along_x(rows_in.at[pl.ds(0, 3)], lambda to: rows_in.at[me.x], rows_in.at[me.x])
     start_all(row_copies)
+    arrive_all(student_stages[0])
+    start_all(student_stages[1])
     arrive_all(row_copies)
 
     def row_inverse(quarters):
@@ -431,14 +398,13 @@
             tb[me.c, me.y, me.z, me.x, :, cols] = normed[me.x, :, cols]
     start_all(teacher_stages[0])
 
-    for n in range(3):
-        tab_copy(n)[1].wait_recv()
-    for group in range(4):
-        table = tab[group]
+    arrive_all([tables])
+    for part in range(4):
+        table = tab[part]
         for row, col in ((0, lab_col), (1, wgt_col)):
             turned = jnp.broadcast_to(table[row : row + 1, :], (LANES, LANES)).T
             for m, (c, y, z) in enumerate(PIECES):
-                if (y % 2) * 2 + c == group:
+                if (y % 2) * 2 + c == part:
                     j = (y // 2) * 4 + z
                     col[m * 16 : (m + 1) * 16, :] = turned[j * 16 : (j + 1) * 16, :]
     g[:, 2:4, 2:4] = jnp.zeros((2, 2, 2, 4, 16, QS), BF16)
@@ -523,21 +489,21 @@
             label += v[5:6]
         return [t_max, t_sum, cross, s_max, s_sum, label, values[0][6:7]]
 
-    for n, axis in enumerate("cxyz"):
-        copies = []
-        for k in (1,) if axis == "c" else (1, 2, 3):
-            sems = (st_send.at[n, k - 1], st_recv.at[n, k - 1])
-            dst = stat_in.at[n, k - 1]
-            to = me.sibling() if axis == "c" else me.along(axis, me.shifted(axis, k))
-            copy = remote(stat.at[n], dst, *sems, to)
-            copies.append((copy, copy))
-        start_all(copies)
-        arrive_all(copies)
-        values = [stat[n]] + [stat_in[n, k] for k in range(len(copies))]
+    for n, axes in enumerate(("c", "xz", "y")):
+        if axes == "c":
+            peers = [me.sibling()]
+        else:
+            peers = [me.to(**sent) for sent, heard in me.offsets(axes)]
+        made = group(stat_in.at[n, pl.ds(0, len(peers))])
+        for k, to in enumerate(peers):
+            put(made, stat.at[n], stat_in.at[n, k], to)
+        start_all([made])
+        arrive_all([made])
+        values = [stat[n]] + [stat_in[n, k] for k in range(len(peers))]
         for i, line in enumerate(merged(values)):
             stat[n + 1, i : i + 1, :] = line
 
-    end = stat[4]
+    end = stat[3]
     t_whole = end[0:1] + jnp.log(end[1:2])
     s_whole = end[3:4] + jnp.log(end[4:5])
     divergence = end[2:3] / end[1:2] - t_whole + s_whole
@@ -563,71 +529,54 @@
         scale = LOSS_SCALE * wgt_col[rows, 0:1]
         lg[rows, :] = (scale * ((1.0 + BETA) * s_prob - t_prob - BETA * hit)).astype(BF16)
 
-    def quarter(k, core):
+    def quarter(k):
         q = me.shifted("x", k)
-        return lax.dot_general(
-            lg[pl.ds(pl.multiple_of(core * HALF, HALF), HALF), :],
+        share[k % 2] = lax.dot_general(
+            lg[...],
             w_s[pl.ds(pl.multiple_of(q * QS, QS), QS), :],
             (((1,), (1,)), ((), ())),
             preferred_element_type=F32,
         )
 
+    def core_rows(k, core, at, count):
+        return share[k % 2, pl.ds(pl.multiple_of(core * HALF + at, 64), count), :]
+
+    reduce_copies = [group(rr0[0]), group(rr0[1]), group(rr_x.at[:, pl.ds(0, 3)])]
+
     def first_reduce(k):
         q = me.shifted("x", k)
-        copies = []
         for p, (lo, width, axis, then) in enumerate(PARTS_G):
             for n, (sent, heard) in enumerate(me.offsets(axis)):
                 where = {a: pl.ds(sent[a], 1) if a in sent else slice(None) for a in "yz"}
-                copy = remote(
-                    g.at[me.c, where["y"], where["z"], q, :, pl.ds(lo, width)],
-                    rr0[p].at[n, k - 1],
-                    rs_send.at[p, n, k - 1],
-                    rs_recv.at[p, n, k - 1],
-                    me.to(**sent),
-                )
-                copies.append((copy, copy))
+                src = g.at[me.c, where["y"], where["z"], q, :, pl.ds(lo, width)]
+                put(reduce_copies[p], src, rr0[p].at[n, k - 1], me.to(**sent))
         if k < 4:
-            for i, (y, z) in enumerate(LIVE):
-                copy = remote(
-                    g.at[me.c, y, z, q, :, pl.ds(LO_X, W_X)],
-                    rr_x.at[k - 1, y, z],
-                    rx_send.at[k - 1, i],
-                    rx_recv.at[k - 1, i],
-                    me.along("x", q),
-                )
-                copies.append((copy, copy))
-        return copies
-
-    core_copies, reduce_copies = [], []
+            for y, z in LIVE:
+                src = g.at[me.c, y, z, q, :, pl.ds(LO_X, W_X)]
+                put(reduce_copies[2], src, rr_x.at[k - 1, y, z], me.along("x", q))
+
+    core_copies = []
     for k in range(1, 6):
         if k < 5:
             q = me.shifted("x", k)
-            share = quarter(k, 1 - me.c).astype(BF16)
-            g[1 - me.c, 0:2, :, q] = share[0:128].reshape(2, 4, 16, QS)
-            g[1 - me.c, 2:4, 0:2, q] = share[128:192].reshape(2, 2, 16, QS)
-            copies = []
-            for i, (y, z) in enumerate(LIVE):
-                copy = remote(
-                    g.at[1 - me.c, y, z, q],
-                    core_in.at[k - 1, y, z],
-                    cs_send.at[k - 1, i],
-                    cs_recv.at[k - 1, i],
-                    me.sibling(),
-                )
-                copies.append((copy, copy))
-            start_all(copies)
-            core_copies.append(copies)
+            quarter(k)
+            theirs = 1 - me.c
+            g[theirs, 0:2, :, q] = core_rows(k, theirs, 0, 128).astype(BF16).reshape(2, 4, 16, QS)
+            g[theirs, 2:4, 0:2, q] = core_rows(k, theirs, 128, 64).astype(BF16).reshape(2, 2, 16, QS)
+            made = group(core_in.at[k - 1, pl.ds(0, 3)])
+            for y, z in LIVE:
+                put(made, g.at[theirs, y, z, q], core_in.at[k - 1, y, z], me.sibling())
+            start_all([made])
+            core_copies.append(made)
         if k > 1:
             q = me.shifted("x", k - 1)
-            share = quarter(k - 1, me.c)
-            arrive_all(core_copies[k - 2])
+            arrive_all([core_copies[k - 2]])
             other = core_in[k - 2, 0:2].reshape(128, QS).astype(F32)
-            g[me.c, 0:2, :, q] = (share[0:128] + other).astype(BF16).reshape(2, 4, 16, QS)
+            g[me.c, 0:2, :, q] = (core_rows(k - 1, me.c, 0, 128) + other).astype(BF16).reshape(2, 4, 16, QS)
             other = core_in[k - 2, 2:4, 0:2].reshape(64, QS).astype(F32)
-            g[me.c, 2:4, 0:2, q] = (share[128:192] + other).astype(BF16).reshape(2, 2, 16, QS)
-            copies = first_reduce(k - 1)
-            start_all(copies)
-            reduce_copies += copies
+            g[me.c, 2:4, 0:2, q] = (core_rows(k - 1, me.c, 128, 64) + other).astype(BF16).reshape(2, 2, 16, QS)
+            first_reduce(k - 1)
+            start_all(reduce_copies)
 
     arrive_all(reduce_copies)
     for p, (lo, width, axis, then) in enumerate(PARTS_G):
@@ -655,27 +604,15 @@
                     whole = whole + rr_x[n, y, z].astype(F32)
                 g[me.c, y, z, me.x, :, cols_x] = whole.astype(BF16)
 
-    second = []
+    second = [group(rr1), group(rr2)]
     for p, (lo, width, axis, then) in enumerate(PARTS_G):
         for n, (sent, heard) in enumerate(me.offsets(then)):
             at = {axis: me.at(axis), **sent}
-            copy = remote(
-                g.at[me.c, at["y"], at["z"], :, :, pl.ds(lo, width)],
-                rr1.at[p, n],
-                r1_send.at[p, n],
-                r1_recv.at[p, n],
-                me.to(**sent),
-            )
-            second.append((copy, copy))
+            src = g.at[me.c, at["y"], at["z"], :, :, pl.ds(lo, width)]
+            put(second[0], src, rr1.at[p, n], me.to(**sent))
     for n, (sent, heard) in enumerate(me.offsets("yz")):
-        copy = remote(
-            g.at[me.c, sent["y"], sent["z"], me.x, :, pl.ds(LO_X, W_X)],
-            rr2.at[n],
-            r2_send.at[n],
-            r2_recv.at[n],
-            me.to(**sent),
-        )
-        second.append((copy, copy))
+        src = g.at[me.c, sent["y"], sent["z"], me.x, :, pl.ds(LO_X, W_X)]
+        put(second[1], src, rr2.at[n], me.to(**sent))
     start_all(second)
     arrive_all(second)
     for p, (lo, width, axis, then) in enumerate(PARTS_G):
@@ -692,8 +629,8 @@
         ng_out[i, :, 4 * W_YZ : 4 * W_YZ + W_X] = whole[4 * i : 4 * i + 4]
 
     ng_in[me.x] = ng_out[me.x]
-    for k in (1, 2, 3):
-        x_copy(4, ng_out, ng_in, k).start()
+    last = along_x(ng_in.at[pl.ds(0, 3)], lambda to: ng_out.at[to], ng_in.at[me.x])
+    start_all(last)
 
     losses = loss_blk[me.c, me.y, me.z]
     mine = jnp.zeros((4, LANES), F32)
@@ -704,8 +641,7 @@
     )
     loss_ref[...] = jnp.sum(jnp.where(diagonal, mine, 0.0), axis=0, keepdims=True)
 
-    for k in (1, 2, 3):
-        x_arrival(4, ng_out, ng_in, k).wait_recv()
+    arrive_all(last)
     norm_parts = []
     for q in range(4):
         cols = slice(q * W_YZ, (q + 1) * W_YZ)
@@ -718,13 +654,18 @@
     grad = inverse * scaled - hidden * (inverse * inverse * inverse) * inner
     grad_ref[...] = jnp.where(live, grad, 0.0)
 
-    for k in (1, 2, 3):
-        x_copy(0, stu_out, stu_in, k).wait_send()
-        x_copy(4, ng_out, ng_in, k).wait_send()
-    for n in range(3):
-        tab_copy(n)[0].wait_send()
-    for sent, unused in opened:
-        sent.wait_send()
+    out_copies = (
+        pltpu.make_async_copy(grad_ref, grad_hbm, out_sem.at[0]),
+        pltpu.make_async_copy(loss_ref, loss_hbm, out_sem.at[1]),
+    )
+    for copy in out_copies:
+        copy.start()
+
+    for made in opened:
+        both_ends(made).wait_send()
+    assert len(opened) == GROUPS
+    for copy in out_copies:
+        copy.wait()
 
 
 def scratch():
@@ -739,6 +680,17 @@
         spots = [1 if a == axis else 4 for a in "yz"]
         rr0.append(vm((3, 4, *spots, 16, width), BF16))
     return {
+        "residual_ref": vm((4, D_T), BF16),
+        "post_ref": vm((D_T,), F32),
+        "final_ref": vm((D_T,), F32),
+        "hidden_ref": vm((4, D_S), BF16),
+        "s_gain_ref": vm((D_S,), F32),
+        "labels_ref": vm((1, LANES), jnp.int32),
+        "lengths_ref": pltpu.SMEM((1, NSEQ), jnp.int32),
+        "grad_ref": vm((4, D_S), F32),
+        "loss_ref": vm((1, LANES), F32),
+        "in_sem": dma((7,)),
+        "out_sem": dma((2,)),
         "w_t": vm((D_T, VOC), BF16),
         "w_s": vm((D_S, VOC), BF16),
         "pb": vm((2, 4, 4, 16, QT), BF16),
@@ -760,11 +712,12 @@
         "t_log": vm((ROWS, VOC), F32),
         "s_log": vm((ROWS, VOC), F32),
         "lg": vm((ROWS, VOC), BF16),
-        "stat": vm((5, 8, ROWS), F32),
-        "stat_in": vm((4, 3, 8, ROWS), F32),
+        "stat": vm((4, 8, ROWS), F32),
+        "stat_in": vm((3, 15, 8, ROWS), F32),
         "back": vm((ROWS, LANES), F32),
         "loss_blk": vm((2, 4, 4, 16, LANES), F32),
         "g": vm((2, 4, 4, 4, 16, QS), BF16),
+        "share": vm((2, ROWS, QS), F32),
         "core_in": vm((4, 4, 4, 16, QS), BF16),
         "rr0": tuple(rr0),
         "rr_x": vm((3, 4, 4, 16, W_X), BF16),
@@ -774,30 +727,7 @@
         "ng_in": vm((4, 4, 4 * W_YZ + W_X), F32),
         "sem_w": dma((2,)),
         "a_own": dma((4,)),
-        "f_send": dma((3, 3)),
-        "f_recv": dma((3, 3)),
-        "h_send": dma((3, 15)),
-        "h_recv": dma((3, 15)),
-        "x_send": dma((5, 3)),
-        "x_recv": dma((5, 3)),
-        "tab_send": dma((3,)),
-        "tab_recv": dma((3,)),
-        "ag_send": dma((2, 3, 3, 15)),
-        "ag_recv": dma((2, 3, 3, 15)),
-        "sib_send": dma((3, 2)),
-        "sib_recv": dma((3, 2)),
-        "st_send": dma((4, 3)),
-        "st_recv": dma((4, 3)),
-        "cs_send": dma((4, 2)),
-        "cs_recv": dma((4, 2)),
-        "rs_send": dma((2, 3, 4)),
-        "rs_recv": dma((2, 3, 4)),
-        "rx_send": dma((3, 2)),
-        "rx_recv": dma((3, 2)),
-        "r1_send": dma((2, 3)),
-        "r1_recv": dma((2, 3)),
-        "r2_send": dma((15,)),
-        "r2_recv": dma((15,)),
+        "pool": dma((2 * GROUPS,)),
     }
 
 
@@ -813,7 +743,6 @@
     labels,
     lengths,
 ):
-    whole = pl.BlockSpec(memory_space=pltpu.VMEM)
     place = pl.BlockSpec(memory_space=pl.ANY)
     spaces = scratch()
     names = list(spaces)
@@ -829,19 +758,8 @@
             jax.ShapeDtypeStruct((4, D_S), F32),
             jax.ShapeDtypeStruct((1, LANES), F32),
         ),
-        in_specs=[
-            place,
-            whole,
-            whole,
-            whole,
-            place,
-            whole,
-            whole,
-            place,
-            whole,
-            pl.BlockSpec(memory_space=pltpu.SMEM),
-        ],
-        out_specs=(whole, whole),
+        in_specs=[place] * 10,
+        out_specs=(place, place),
         scratch_shapes=leaves,
         compiler_params=pltpu.CompilerParams(
             collective_id=0, has_side_effects=True, vmem_limit_bytes=60 * 2**20

time: 109 us -> 99.6 us (0.914)
  Pallas kernels: 106 us -> 96.2 us
    pallas_call x1, Pallas kernels: 106 us -> 96.2 us  [shards(): pl.pallas_call(body, out_shape=(jax.ShapeDtypeStruct((4, D_S), F32), jax....]
where the time goes in v4:
time: 99.6 us; the launch traced here: 99.4 us
  Pallas kernels  96.2 us (97%)
  local copies, waits for them, and re-layouts  2.56 us (3%)
    pallas_call x1, Pallas kernels, shards(): pl.pallas_call(body, out_shape=(jax.ShapeDtypeStruct((4, D_S), F32), jax....  96.2 us

profile of v4, /device:TPU:0, one launch (start us, length us, event | category | flops | bytes accessed | tf_op | source)
XLA Modules:
  0.0 99.4 jit_solution(4060811097227739247)
XLA Ops:
  0.6 96.2 %distill.1 = (f32[4,3584]{1,0:T(4,128)}, f32[1,128]{1,0:T(1,128)}) custom-call(bf16[2,4,16,4608]{3,2,1,0:T(8,128)(2,1)} %bitcast.4, bf16[4,4608]{1,0:T(4,128)(2,1)} %refs_1_.1, f32[4608]{0:T(1024)} %refs_2_.1, f32[4608]{0:T(1024)} %refs_3_.1, bf16[4608,1024]{1,0:T(8,128)(2,1)} %refs_4_.1, bf16[4,3584]{1,0:T(4,128)(2,1)} %refs_5_.1, f32[3584]{0:T(1024)} %refs_6_.1, ...), custom_call_target="tpu_custom_call" | custom-call | tf_op jit(solution)/shard_map/distill/pallas_call | solution.py:755
  96.8 1.1 %slice_bitcast_fusion = f32[4]{0:T(128)} fusion(f32[1,128]{1,0:T(1,128)} %get-tuple-element.5), kind=kLoop, calls=%fused_computation | loop fusion | bytes 32 | tf_op jit(solution)/shard_map/squeeze | solution.py:780
  98.0 1.4 %copy.13 = f32[4,3584]{1,0:T(4,128)} copy(f32[4,3584]{1,0:T(4,128)} %get-tuple-element.8) | data formatting | bytes 114688

commit v5 on v4

--- a/solution.py
+++ b/solution.py
@@ -38,7 +38,7 @@
 PARTS_G = ((0, 256, "z", "y"), (256, 256, "y", "z"))
 LO_X, W_X = (512, 384)
 W_YZ = 512
-GROUPS = 40
+GROUPS = 42
 
 
 def live_pieces():
@@ -316,12 +316,12 @@
                 put(made, src, src, me.to(**sent))
         return made
 
-    def swap(buf):
-        made = group(buf.at[0, pl.ds(0, 3)])
+    def swap(buf, cols):
+        made = group(buf.at[0, pl.ds(0, 3), :, :, :, cols])
         for y, z in LIVE:
-            own = buf.at[me.c, y, z]
+            own = buf.at[me.c, y, z, :, :, cols]
             put(made, own, own, me.sibling())
-        return [made]
+        return made
 
     student_stages, teacher_stages = [[], [], []], [[], []]
     for stage in range(3):
@@ -332,7 +332,15 @@
         whole = second_in[2] if len(first) == 2 else None
         teacher_stages[0].append(one_part(tb, lo, width, first, done, whole))
         teacher_stages[1].append(one_part(tb, lo, width, second, done + first))
-    student_swap, teacher_swap = swap(sb), swap(tb)
+    student_swap = [swap(sb, pl.ds(0, QS))]
+    teacher_swap = [swap(tb, pl.ds(part[0], part[1])) for part in PARTS_T]
+
+    arrive_all(student_copies)
+    for i in range(4):
+        asm_s[4 * i : 4 * i + 4, :] = stu_in[i].astype(F32)
+    sb[me.c, me.y, me.z, me.x] = asm_s[...].astype(BF16)
+    start_all(student_stages[0])
+
 
     arrive_all(first_stage)
     for p, (lo, width, axis, plane) in enumerate(PARTS_A):
@@ -353,12 +361,8 @@
             pb[at["h"], at["z"], at["x"], :, cols] = whole.astype(BF16)
 
     start_all(second_stage)
-    arrive_all(student_copies)
-    for i in range(4):
-        asm_s[4 * i : 4 * i + 4, :] = stu_in[i].astype(F32)
-    sb[me.c, me.y, me.z, me.x] = asm_s[...].astype(BF16)
-    start_all(student_stages[0])
-
+    arrive_all(student_stages[0])
+    start_all(student_stages[1])
     arrive_all(residual_copies)
     for q in range(4):
         for i in range(4):
@@ -372,8 +376,8 @@
 
     row_copies = along_x(rows_in.at[pl.ds(0, 3)], lambda to: rows_in.at[me.x], rows_in.at[me.x])
     start_all(row_copies)
-    arrive_all(student_stages[0])
-    start_all(student_stages[1])
+    arrive_all(student_stages[1])
+    start_all(student_stages[2])
     arrive_all(row_copies)
 
     def row_inverse(quarters):
@@ -410,10 +414,8 @@
     g[:, 2:4, 2:4] = jnp.zeros((2, 2, 2, 4, 16, QS), BF16)
     loss_blk[:, 2:4, 2:4] = jnp.zeros((2, 2, 2, 16, LANES), F32)
 
-    arrive_all(student_stages[1])
     arrive_all(teacher_stages[0])
     start_all(teacher_stages[1])
-    start_all(student_stages[2])
 
     def logits(buf, head, out, width, core):
         rows = pl.ds(pl.multiple_of(core * HALF, HALF), HALF)
@@ -435,42 +437,56 @@
                 acc = term if acc is None else acc + term
             out[rows, cols] = acc
 
-    load_t.wait()
-    arrive_all(teacher_stages[1])
-    start_all(teacher_swap)
-    logits(tb, w_t, t_log, QT, me.c)
+    first_col = (position * VOC).astype(F32)
+
+    def columns():
+        return lax.broadcasted_iota(jnp.int32, (32, VOC), 1).astype(F32) + first_col
+
+    lanes = lax.broadcasted_iota(jnp.int32, (32, LANES), 1)
+
+    def student_stats():
+        @pl.loop(0, ROWS // 32)
+        def _(r):
+            rows = pl.ds(pl.multiple_of(r * 32, 32), 32)
+            s = s_log[rows, :]
+            s_max = jnp.max(s, axis=1, keepdims=True)
+            s_sum = jnp.sum(jnp.exp(s - s_max), axis=1, keepdims=True)
+            hit = columns() == lab_col[rows, 0:1]
+            value = jnp.sum(jnp.where(hit, s, 0.0), axis=1, keepdims=True)
+            held = wgt_col[rows, :]
+            for n, one in ((3, s_max), (4, s_sum), (5, value)):
+                held = jnp.where(lanes == n, one, held)
+            back[rows, :] = held
+
+    def teacher_stats():
+        @pl.loop(0, ROWS // 32)
+        def _(r):
+            rows = pl.ds(pl.multiple_of(r * 32, 32), 32)
+            t = t_log[rows, :]
+            t_max = jnp.max(t, axis=1, keepdims=True)
+            t_exp = jnp.exp(t - t_max)
+            t_sum = jnp.sum(t_exp, axis=1, keepdims=True)
+            cross = jnp.sum(t_exp * (t - s_log[rows, :]), axis=1, keepdims=True)
+            held = back[rows, :]
+            for n, one in ((0, t_max), (1, t_sum), (2, cross)):
+                held = jnp.where(lanes == n, one, held)
+            back[rows, :] = held
+
+    load_s.wait()
     arrive_all(student_stages[2])
     start_all(student_swap)
-    arrive_all(teacher_swap)
-    logits(tb, w_t, t_log, QT, 1 - me.c)
-    load_s.wait()
     logits(sb, w_s, s_log, QS, me.c)
     arrive_all(student_swap)
     logits(sb, w_s, s_log, QS, 1 - me.c)
-
-    first_col = (position * VOC).astype(F32)
-
-    def columns():
-        return lax.broadcasted_iota(jnp.int32, (32, VOC), 1).astype(F32) + first_col
-
-    lanes = lax.broadcasted_iota(jnp.int32, (32, LANES), 1)
-
-    @pl.loop(0, ROWS // 32)
-    def _(r):
-        rows = pl.ds(pl.multiple_of(r * 32, 32), 32)
-        t, s = t_log[rows, :], s_log[rows, :]
-        t_max = jnp.max(t, axis=1, keepdims=True)
-        s_max = jnp.max(s, axis=1, keepdims=True)
-        t_exp = jnp.exp(t - t_max)
-        t_sum = jnp.sum(t_exp, axis=1, keepdims=True)
-        cross = jnp.sum(t_exp * (t - s), axis=1, keepdims=True)
-        s_sum = jnp.sum(jnp.exp(s - s_max), axis=1, keepdims=True)
-        hit = columns() == lab_col[rows, 0:1]
-        value = jnp.sum(jnp.where(hit, s, 0.0), axis=1, keepdims=True)
-        held = wgt_col[rows, :]
-        for n, one in enumerate((t_max, t_sum, cross, s_max, s_sum, value)):
-            held = jnp.where(lanes == n, one, held)
-        back[rows, :] = held
+    student_stats()
+    load_t.wait()
+    for p in (2, 0, 1):
+        arrive_all([teacher_stages[1][p]])
+        start_all([teacher_swap[p]])
+    logits(tb, w_t, t_log, QT, me.c)
+    arrive_all(teacher_swap)
+    logits(tb, w_t, t_log, QT, 1 - me.c)
+    teacher_stats()
 
     for i in range(3):
         turned = back[i * 128 : (i + 1) * 128, :].T

time: 99.6 us -> 95.4 us (0.958)
  Pallas kernels: 96.2 us -> 92 us
    pallas_call x1, Pallas kernels: 96.2 us -> 92 us  [shards(): pl.pallas_call(body, out_shape=(jax.ShapeDtypeStruct((4, D_S), F32), jax....]
where the time goes in v5:
time: 95.4 us; the launch traced here: 95.2 us
  Pallas kernels  92 us (96%)
  local copies, waits for them, and re-layouts  2.56 us (3%)
    pallas_call x1, Pallas kernels, shards(): pl.pallas_call(body, out_shape=(jax.ShapeDtypeStruct((4, D_S), F32), jax....  92 us

profile of v5, /device:TPU:0, one launch (start us, length us, event | category | flops | bytes accessed | tf_op | source)
XLA Modules:
  0.0 95.2 jit_solution(12198499853334747138)
XLA Ops:
  0.6 92.0 %distill.1 = (f32[4,3584]{1,0:T(4,128)}, f32[1,128]{1,0:T(1,128)}) custom-call(bf16[2,4,16,4608]{3,2,1,0:T(8,128)(2,1)} %bitcast.4, bf16[4,4608]{1,0:T(4,128)(2,1)} %refs_1_.1, f32[4608]{0:T(1024)} %refs_2_.1, f32[4608]{0:T(1024)} %refs_3_.1, bf16[4608,1024]{1,0:T(8,128)(2,1)} %refs_4_.1, bf16[4,3584]{1,0:T(4,128)(2,1)} %refs_5_.1, f32[3584]{0:T(1024)} %refs_6_.1, ...), custom_call_target="tpu_custom_call" | custom-call | tf_op jit(solution)/shard_map/distill/pallas_call | solution.py:771
  92.6 1.1 %slice_bitcast_fusion = f32[4]{0:T(128)} fusion(f32[1,128]{1,0:T(1,128)} %get-tuple-element.5), kind=kLoop, calls=%fused_computation | loop fusion | bytes 32 | tf_op jit(solution)/shard_map/squeeze | solution.py:796
  93.8 1.4 %copy.13 = f32[4,3584]{1,0:T(4,128)} copy(f32[4,3584]{1,0:T(4,128)} %get-tuple-element.8) | data formatting | bytes 114688

commit v6 on v5

--- a/solution.py
+++ b/solution.py
@@ -85,6 +85,10 @@
                 sent = {a: self.shifted(a, k) for a, k in zip(axes, ks)}
                 heard = {a: self.shifted(a, n - k) for a, k, n in zip(axes, ks, sizes)}
                 yield (sent, heard)
+
+    def across(self, k):
+        to = self.shifted("y", k)
+        return (lax.rem(to, 2), 1 - self.c, lax.div(to, 2), self.z, self.x)
 
     def sibling(self):
         return (self.y_lo, 1 - self.c, self.y_hi, self.z, self.x)
@@ -194,7 +198,7 @@
     for k in (1, 2, 3):
         near += [me.to(x=me.shifted("x", k), z=me.shifted("z", n)) for n in (1, 2, 3)]
         near += [me.to(x=me.shifted("x", k), h=1 - me.y_hi)]
-    near += [me.sibling(), (1 - me.y_lo, 1 - me.c, me.y_hi, me.z, me.x)]
+    near += [me.sibling()] + [me.across(k) for k in (1, 2, 3)]
     for to in near:
         pl.semaphore_signal(barrier, inc=1, device_id=to, device_id_type=MESH)
     pl.semaphore_wait(barrier, len(near))
@@ -342,8 +346,8 @@
     start_all(student_stages[0])
 
 
-    arrive_all(first_stage)
     for p, (lo, width, axis, plane) in enumerate(PARTS_A):
+        arrive_all([first_stage[p]])
         came = first_in[p]
         count = came.shape[0]
 
@@ -360,15 +364,16 @@
                 whole = whole + came[i, slot["h"], slot["z"], slot["x"]].astype(F32)
             pb[at["h"], at["z"], at["x"], :, cols] = whole.astype(BF16)
 
-    start_all(second_stage)
+        start_all([second_stage[p]])
+
     arrive_all(student_stages[0])
     start_all(student_stages[1])
     arrive_all(residual_copies)
     for q in range(4):
         for i in range(4):
             asm_t[q, 4 * i : 4 * i + 4, :] = res_in[i, :, q * QT : (q + 1) * QT].astype(F32)
-    arrive_all(second_stage)
     for p, (lo, width, axis, plane) in enumerate(PARTS_A):
+        arrive_all([second_stage[p]])
         whole = pb[me.y_hi, me.z, me.x, :, lo : lo + width].astype(F32)
         for n in range(second_in[p].shape[0]):
             whole = whole + second_in[p][n].astype(F32)
@@ -414,8 +419,9 @@
     g[:, 2:4, 2:4] = jnp.zeros((2, 2, 2, 4, 16, QS), BF16)
     loss_blk[:, 2:4, 2:4] = jnp.zeros((2, 2, 2, 16, LANES), F32)
 
-    arrive_all(teacher_stages[0])
-    start_all(teacher_stages[1])
+    for p in range(3):
+        arrive_all([teacher_stages[0][p]])
+        start_all([teacher_stages[1][p]])
 
     def logits(buf, head, out, width, core):
         rows = pl.ds(pl.multiple_of(core * HALF, HALF), HALF)
@@ -505,11 +511,12 @@
             label += v[5:6]
         return [t_max, t_sum, cross, s_max, s_sum, label, values[0][6:7]]
 
-    for n, axes in enumerate(("c", "xz", "y")):
-        if axes == "c":
-            peers = [me.sibling()]
+    for n, axes in enumerate(("xz", "yc")):
+        if axes == "xz":
+            peers = [me.to(**sent) for sent, heard in me.offsets(axes)]
         else:
-            peers = [me.to(**sent) for sent, heard in me.offsets(axes)]
+            peers = [me.along("y", me.shifted("y", k)) for k in (1, 2, 3)]
+            peers += [me.sibling()] + [me.across(k) for k in (1, 2, 3)]
         made = group(stat_in.at[n, pl.ds(0, len(peers))])
         for k, to in enumerate(peers):
             put(made, stat.at[n], stat_in.at[n, k], to)
@@ -519,7 +526,7 @@
         for i, line in enumerate(merged(values)):
             stat[n + 1, i : i + 1, :] = line
 
-    end = stat[3]
+    end = stat[2]
     t_whole = end[0:1] + jnp.log(end[1:2])
     s_whole = end[3:4] + jnp.log(end[4:5])
     divergence = end[2:3] / end[1:2] - t_whole + s_whole
@@ -594,9 +601,10 @@
             first_reduce(k - 1)
             start_all(reduce_copies)
 
-    arrive_all(reduce_copies)
+    second = [group(rr1.at[0]), group(rr1.at[1]), group(rr2)]
     for p, (lo, width, axis, then) in enumerate(PARTS_G):
         cols = slice(lo, lo + width)
+        arrive_all([reduce_copies[p]])
         for k in range(1, 5):
             q = me.shifted("x", k)
 
@@ -609,7 +617,14 @@
                     whole = whole + rr0[p][n, k - 1, slot["y"], slot["z"]].astype(F32)
                 g[me.c, at["y"], at["z"], q, :, cols] = whole.astype(BF16)
 
+        for n, (sent, heard) in enumerate(me.offsets(then)):
+            at = {axis: me.at(axis), **sent}
+            src = g.at[me.c, at["y"], at["z"], :, :, pl.ds(lo, width)]
+            put(second[p], src, rr1.at[p, n], me.to(**sent))
+        start_all([second[p]])
+
     cols_x = slice(LO_X, LO_X + W_X)
+    arrive_all([reduce_copies[2]])
     for ys, zs in (((0, 1), 4), ((2, 3), 2)):
         for y in ys:
 
@@ -620,24 +635,19 @@
                     whole = whole + rr_x[n, y, z].astype(F32)
                 g[me.c, y, z, me.x, :, cols_x] = whole.astype(BF16)
 
-    second = [group(rr1), group(rr2)]
-    for p, (lo, width, axis, then) in enumerate(PARTS_G):
-        for n, (sent, heard) in enumerate(me.offsets(then)):
-            at = {axis: me.at(axis), **sent}
-            src = g.at[me.c, at["y"], at["z"], :, :, pl.ds(lo, width)]
-            put(second[0], src, rr1.at[p, n], me.to(**sent))
     for n, (sent, heard) in enumerate(me.offsets("yz")):
         src = g.at[me.c, sent["y"], sent["z"], me.x, :, pl.ds(LO_X, W_X)]
-        put(second[1], src, rr2.at[n], me.to(**sent))
-    start_all(second)
-    arrive_all(second)
+        put(second[2], src, rr2.at[n], me.to(**sent))
+    start_all([second[2]])
     for p, (lo, width, axis, then) in enumerate(PARTS_G):
+        arrive_all([second[p]])
         for q in range(4):
             whole = g[me.c, me.y, me.z, q, :, lo : lo + width].astype(F32)
             for n in range(3):
                 whole = whole + rr1[p, n, q].astype(F32)
             for i in range(4):
                 ng_out[i, :, q * W_YZ + lo : q * W_YZ + lo + width] = whole[4 * i : 4 * i + 4]
+    arrive_all([second[2]])
     whole = g[me.c, me.y, me.z, me.x, :, cols_x].astype(F32)
     for n in range(15):
         whole = whole + rr2[n].astype(F32)
@@ -728,8 +738,8 @@
         "t_log": vm((ROWS, VOC), F32),
         "s_log": vm((ROWS, VOC), F32),
         "lg": vm((ROWS, VOC), BF16),
-        "stat": vm((4, 8, ROWS), F32),
-        "stat_in": vm((3, 15, 8, ROWS), F32),
+        "stat": vm((3, 8, ROWS), F32),
+        "stat_in": vm((2, 15, 8, ROWS), F32),
         "back": vm((ROWS, LANES), F32),
         "loss_blk": vm((2, 4, 4, 16, LANES), F32),
         "g": vm((2, 4, 4, 4, 16, QS), BF16),

time: 95.4 us -> 93.7 us (0.982)
  Pallas kernels: 92 us -> 90.3 us
    pallas_call x1, Pallas kernels: 92 us -> 90.3 us  [shards(): pl.pallas_call(body, out_shape=(jax.ShapeDtypeStruct((4, D_S), F32), jax....]
where the time goes in v6:
time: 93.7 us; the launch traced here: 93.5 us
  Pallas kernels  90.3 us (96%)
  local copies, waits for them, and re-layouts  2.56 us (3%)
    pallas_call x1, Pallas kernels, shards(): pl.pallas_call(body, out_shape=(jax.ShapeDtypeStruct((4, D_S), F32), jax....  90.3 us

profile of v6, /device:TPU:0, one launch (start us, length us, event | category | flops | bytes accessed | tf_op | source)
XLA Modules:
  0.0 93.5 jit_solution(5819124406288015400)
XLA Ops:
  0.6 90.3 %distill.1 = (f32[4,3584]{1,0:T(4,128)}, f32[1,128]{1,0:T(1,128)}) custom-call(bf16[2,4,16,4608]{3,2,1,0:T(8,128)(2,1)} %bitcast.4, bf16[4,4608]{1,0:T(4,128)(2,1)} %refs_1_.1, f32[4608]{0:T(1024)} %refs_2_.1, f32[4608]{0:T(1024)} %refs_3_.1, bf16[4608,1024]{1,0:T(8,128)(2,1)} %refs_4_.1, bf16[4,3584]{1,0:T(4,128)(2,1)} %refs_5_.1, f32[3584]{0:T(1024)} %refs_6_.1, ...), custom_call_target="tpu_custom_call" | custom-call | tf_op jit(solution)/shard_map/distill/pallas_call | solution.py:781
  91.0 1.1 %slice_bitcast_fusion = f32[4]{0:T(128)} fusion(f32[1,128]{1,0:T(1,128)} %get-tuple-element.5), kind=kLoop, calls=%fused_computation | loop fusion | bytes 32 | tf_op jit(solution)/shard_map/squeeze | solution.py:806
  92.1 1.4 %copy.13 = f32[4,3584]{1,0:T(4,128)} copy(f32[4,3584]{1,0:T(4,128)} %get-tuple-element.8) | data formatting | bytes 114688

commit v7 on v6

--- a/solution.py
+++ b/solution.py
@@ -169,6 +169,16 @@
 
     load_s = pltpu.make_async_copy(s_head_ref, w_s, sem_w.at[0])
     load_t = pltpu.make_async_copy(t_head_ref, w_t, sem_w.at[1])
+    barrier = pltpu.get_barrier_semaphore()
+    near = [me.to(**sent) for sent, heard in me.offsets("yz")]
+    near += [me.along("x", me.shifted("x", k)) for k in (1, 2, 3)]
+    for k in (1, 2, 3):
+        near += [me.to(x=me.shifted("x", k), z=me.shifted("z", n)) for n in (1, 2, 3)]
+        near += [me.to(x=me.shifted("x", k), h=1 - me.y_hi)]
+    near += [me.sibling()] + [me.across(k) for k in (1, 2, 3)]
+    for to in near:
+        pl.semaphore_signal(barrier, inc=1, device_id=to, device_id_type=MESH)
+
     small_copies = []
     for n, (src, dst) in enumerate(
         (
@@ -192,15 +202,6 @@
         copy.start()
         own_copies.append(copy)
 
-    barrier = pltpu.get_barrier_semaphore()
-    near = [me.to(**sent) for sent, heard in me.offsets("yz")]
-    near += [me.along("x", me.shifted("x", k)) for k in (1, 2, 3)]
-    for k in (1, 2, 3):
-        near += [me.to(x=me.shifted("x", k), z=me.shifted("z", n)) for n in (1, 2, 3)]
-        near += [me.to(x=me.shifted("x", k), h=1 - me.y_hi)]
-    near += [me.sibling()] + [me.across(k) for k in (1, 2, 3)]
-    for to in near:
-        pl.semaphore_signal(barrier, inc=1, device_id=to, device_id_type=MESH)
     pl.semaphore_wait(barrier, len(near))
 
     opened = []
@@ -554,7 +555,7 @@
 
     def quarter(k):
         q = me.shifted("x", k)
-        share[k % 2] = lax.dot_general(
+        share[k % 3] = lax.dot_general(
             lg[...],
             w_s[pl.ds(pl.multiple_of(q * QS, QS), QS), :],
             (((1,), (1,)), ((), ())),
@@ -562,7 +563,7 @@
         )
 
     def core_rows(k, core, at, count):
-        return share[k % 2, pl.ds(pl.multiple_of(core * HALF + at, 64), count), :]
+        return share[k % 3, pl.ds(pl.multiple_of(core * HALF + at, 64), count), :]
 
     reduce_copies = [group(rr0[0]), group(rr0[1]), group(rr_x.at[:, pl.ds(0, 3)])]
 
@@ -579,7 +580,7 @@
                 put(reduce_copies[2], src, rr_x.at[k - 1, y, z], me.along("x", q))
 
     core_copies = []
-    for k in range(1, 6):
+    for k in range(1, 7):
         if k < 5:
             q = me.shifted("x", k)
             quarter(k)
@@ -591,14 +592,14 @@
                 put(made, g.at[theirs, y, z, q], core_in.at[k - 1, y, z], me.sibling())
             start_all([made])
             core_copies.append(made)
-        if k > 1:
-            q = me.shifted("x", k - 1)
-            arrive_all([core_copies[k - 2]])
-            other = core_in[k - 2, 0:2].reshape(128, QS).astype(F32)
-            g[me.c, 0:2, :, q] = (core_rows(k - 1, me.c, 0, 128) + other).astype(BF16).reshape(2, 4, 16, QS)
-            other = core_in[k - 2, 2:4, 0:2].reshape(64, QS).astype(F32)
-            g[me.c, 2:4, 0:2, q] = (core_rows(k - 1, me.c, 128, 64) + other).astype(BF16).reshape(2, 2, 16, QS)
-            first_reduce(k - 1)
+        if k > 2:
+            q = me.shifted("x", k - 2)
+            arrive_all([core_copies[k - 3]])
+            other = core_in[k - 3, 0:2].reshape(128, QS).astype(F32)
+            g[me.c, 0:2, :, q] = (core_rows(k - 2, me.c, 0, 128) + other).astype(BF16).reshape(2, 4, 16, QS)
+            other = core_in[k - 3, 2:4, 0:2].reshape(64, QS).astype(F32)
+            g[me.c, 2:4, 0:2, q] = (core_rows(k - 2, me.c, 128, 64) + other).astype(BF16).reshape(2, 2, 16, QS)
+            first_reduce(k - 2)
             start_all(reduce_copies)
 
     second = [group(rr1.at[0]), group(rr1.at[1]), group(rr2)]
@@ -743,7 +744,7 @@
         "back": vm((ROWS, LANES), F32),
         "loss_blk": vm((2, 4, 4, 16, LANES), F32),
         "g": vm((2, 4, 4, 4, 16, QS), BF16),
-        "share": vm((2, ROWS, QS), F32),
+        "share": vm((3, ROWS, QS), F32),
         "core_in": vm((4, 4, 4, 16, QS), BF16),
         "rr0": tuple(rr0),
         "rr_x": vm((3, 4, 4, 16, W_X), BF16),

time: 93.7 us -> 94.1 us (level)
  no operation moved by 1% of the time
where the time goes in v7:
time: 94.1 us; the launch traced here: 93.9 us
  Pallas kernels  90.7 us (96%)
  local copies, waits for them, and re-layouts  2.56 us (3%)
    pallas_call x1, Pallas kernels, shards(): pl.pallas_call(body, out_shape=(jax.ShapeDtypeStruct((4, D_S), F32), jax....  90.7 us

profile of v7, /device:TPU:0, one launch (start us, length us, event | category | flops | bytes accessed | tf_op | source)
XLA Modules:
  0.0 93.9 jit_solution(4946260001941890458)
XLA Ops:
  0.6 90.7 %distill.1 = (f32[4,3584]{1,0:T(4,128)}, f32[1,128]{1,0:T(1,128)}) custom-call(bf16[2,4,16,4608]{3,2,1,0:T(8,128)(2,1)} %bitcast.4, bf16[4,4608]{1,0:T(4,128)(2,1)} %refs_1_.1, f32[4608]{0:T(1024)} %refs_2_.1, f32[4608]{0:T(1024)} %refs_3_.1, bf16[4608,1024]{1,0:T(8,128)(2,1)} %refs_4_.1, bf16[4,3584]{1,0:T(4,128)(2,1)} %refs_5_.1, f32[3584]{0:T(1024)} %refs_6_.1, ...), custom_call_target="tpu_custom_call" | custom-call | tf_op jit(solution)/shard_map/distill/pallas_call | solution.py:782
  91.4 1.1 %slice_bitcast_fusion = f32[4]{0:T(128)} fusion(f32[1,128]{1,0:T(1,128)} %get-tuple-element.5), kind=kLoop, calls=%fused_computation | loop fusion | bytes 32 | tf_op jit(solution)/shard_map/squeeze | solution.py:807
  92.5 1.4 %copy.13 = f32[4,3584]{1,0:T(4,128)} copy(f32[4,3584]{1,0:T(4,128)} %get-tuple-element.8) | data formatting | bytes 114688
